TPU v7x, 128 devices: a whole 4x4x4 slice. The times are simulated.
128 devices in a mesh: space: 64 (over y, z, x), dp: 2 (over core).
Axes of the slice: x: 4, y: 4, z: 4, core: 2. Of those that a mesh axis runs over, the one named last changes fastest.
Arguments:
- states: bfloat16 [2, 32768, 512], P('dp', 'space'), may hold values from -6 to 6
- cotangent: bfloat16 [2, 32768, 512], P('dp', 'space'), may hold values from -6 to 6
- send_owner: int32 [4096], P('space'), may hold values from 0 to 63, as said below
- line_place: int32 [4096], P('space'), may hold values from 0 to 191, as said below
- gain_attn: float32 [512], replicated, may hold values from 0.1 to 1.9
- w_qkv: bfloat16 [512, 1536], replicated, may hold values from -0.25 to 0.25
- w_out: bfloat16 [512, 512], replicated, may hold values from -0.25 to 0.25
- gain_mlp: float32 [512], replicated, may hold values from 0.1 to 1.9
- w_up: bfloat16 [512, 2048], replicated, may hold values from -0.25 to 0.25
- w_down: bfloat16 [2048, 512], replicated, may hold values from -0.125 to 0.125
Outputs:
- output: bfloat16 [2, 32768, 512], P('dp', 'space')
- grad_states: bfloat16 [2, 32768, 512], P('dp', 'space')
- grad_gain_attn: float32 [512], replicated
- grad_qkv: float32 [512, 1536], replicated
- grad_out: float32 [512, 512], replicated
- grad_gain_mlp: float32 [512], replicated
- grad_up: float32 [512, 2048], replicated
- grad_down: float32 [2048, 512], replicated
Inputs may be any that keep to these rules, and one draw needn't show every extreme that they name: `send_owner`: each block's owner is a space index. Owners' loads are skewed: the busiest attend 3 times the mean number of lines, some over none. Every device sends the same number of blocks to a given owner, at most 3; the busiest owners receive 3 blocks from every device. `line_place`: A block's place is its line's slot at the owner times 4 plus its position in the line. The places of the blocks that one owner receives are 0 to their number less one, each once; the 4 blocks of a line share owner and line slot.
All inputs are finite; a program needn't handle non-finite values.
Results may differ from a plain program's by a relative error of at most 0.017.
Values may be sent and summed in bfloat16 or wider, within the bound.
A program may use at most 128 MiB of HBM per device.

v0:
```python
import math

import jax
import jax.numpy as jnp
from jax import lax
from jax.sharding import PartitionSpec as P

HEADS = 8
SEG = 8
FRAG = 4
PAIR = 1


EPSILON = 1e-05


def norm_rows(values, gain):
    center = values - jnp.mean(values, axis=-1, keepdims=True)
    spread = jnp.mean(center * center, axis=-1, keepdims=True)
    return center * lax.rsqrt(spread + EPSILON) * gain


def gelu_back(pre_act, upstream):
    _, pullback = jax.vjp(jax.nn.gelu, pre_act)
    return pullback(upstream)[0]


def norm_back(values, gain, upstream):
    _, pullback = jax.vjp(norm_rows, values, gain)
    return pullback(upstream)


def contract_rows(left, right):
    return lax.dot_general(
        left, right, (((0,), (0,)), ((), ())), preferred_element_type=jnp.float32
    )


def times_transpose(left, right):
    return lax.dot_general(
        left, right, (((1,), (1,)), ((), ())), preferred_element_type=jnp.float32
    )


def line_weights(queries, keys_in):
    scale = queries.shape[-1] ** (-0.5)
    scores = (
        jnp.einsum("nqhd,nkhd->nhqk", queries, keys_in, preferred_element_type=jnp.float32) * scale
    )
    expo = jnp.exp(scores)
    return expo / jnp.sum(expo, axis=-1, keepdims=True)


def per_device(
    states, cotangent, send_owner, line_place, gain_attn, w_qkv, w_out, gain_mlp, w_up, w_down
):
    width = states.shape[2]
    rows = states.shape[1]
    nspace = lax.axis_size("space")
    total_rows = rows * nspace * lax.axis_size("dp")
    capacity = 3 * PAIR
    slots = nspace * capacity
    nblocks = send_owner.shape[0]
    line_len = FRAG * SEG
    line_count = slots // FRAG
    head_dim = width // HEADS
    scale = head_dim ** (-0.5)
    onehot = (send_owner[:, None] == jnp.arange(nspace, dtype=jnp.int32)[None, :]).astype(jnp.int32)
    ranks = jnp.sum((jnp.cumsum(onehot, axis=0) - onehot) * onehot, axis=1)
    slot_index = send_owner * capacity + ranks
    tags = jnp.full((slots,), slots, jnp.int32).at[slot_index].set(line_place)

    def pack(rows_arr):
        blocks = rows_arr.reshape(nblocks, -1)
        return jnp.zeros((slots, blocks.shape[1]), blocks.dtype).at[slot_index].set(blocks)

    def unpack(buffer):
        return buffer[slot_index].reshape(rows, -1)

    def gather_lines(received, places):
        buffer = jnp.zeros(received.shape, received.dtype).at[places].set(received, mode="drop")
        return buffer.reshape(line_count * line_len, -1)

    def scatter_lines(line_rows, places):
        return jnp.take(line_rows.reshape(slots, -1), places, axis=0, mode="fill", fill_value=0)

    flat = states[0].astype(jnp.float32)
    normed = norm_rows(flat, gain_attn).astype(jnp.bfloat16)
    home_projected = jnp.dot(normed, w_qkv, preferred_element_type=jnp.float32).astype(jnp.bfloat16)
    received, places = (
        lax.all_to_all(pack(home_projected), "space", split_axis=0, concat_axis=0, tiled=True),
        lax.all_to_all(tags, "space", split_axis=0, concat_axis=0, tiled=True),
    )
    projected = gather_lines(received, places)
    heads_shape = (line_count, line_len, HEADS, head_dim)
    queries = projected[:, :width].reshape(heads_shape)
    keys_in = projected[:, width : 2 * width].reshape(heads_shape)
    values_in = projected[:, 2 * width :].reshape(heads_shape)
    probs = line_weights(queries, keys_in)
    rounded = probs.astype(jnp.bfloat16)
    attended = jnp.einsum(
        "nhqk,nkhd->nqhd", rounded, values_in, preferred_element_type=jnp.float32
    ).astype(jnp.bfloat16)
    mixed = unpack(
        lax.all_to_all(
            scatter_lines(attended, places), "space", split_axis=0, concat_axis=0, tiled=True
        )
    )
    hidden = (flat + jnp.dot(mixed, w_out, preferred_element_type=jnp.float32)).astype(jnp.bfloat16)
    hidden32 = hidden.astype(jnp.float32)
    normed_mlp = norm_rows(hidden32, gain_mlp).astype(jnp.bfloat16)
    pre_act = jnp.dot(normed_mlp, w_up, preferred_element_type=jnp.float32)
    activated = jax.nn.gelu(pre_act).astype(jnp.bfloat16)
    output = (hidden32 + jnp.dot(activated, w_down, preferred_element_type=jnp.float32)).astype(
        jnp.bfloat16
    )
    upstream = cotangent[0]
    grad_down = contract_rows(activated, upstream)
    dpre = gelu_back(pre_act, times_transpose(upstream, w_down)).astype(jnp.bfloat16)
    grad_up = contract_rows(normed_mlp, dpre)
    dnormed_mlp = times_transpose(dpre, w_up)
    dhid_norm, grad_gain_mlp = norm_back(hidden32, gain_mlp, dnormed_mlp)
    dhidden = upstream.astype(jnp.float32) + dhid_norm
    dhidden_b = dhidden.astype(jnp.bfloat16)
    grad_out = contract_rows(mixed, dhidden_b)
    dmixed = times_transpose(dhidden_b, w_out).astype(jnp.bfloat16)
    dreceived = lax.all_to_all(pack(dmixed), "space", split_axis=0, concat_axis=0, tiled=True)
    dattended = gather_lines(dreceived, places).reshape(heads_shape)
    dprob = jnp.einsum("nqhd,nkhd->nhqk", dattended, values_in, preferred_element_type=jnp.float32)
    dscore = probs * (dprob - jnp.sum(dprob * probs, axis=-1, keepdims=True))
    dscore_b = (dscore * scale).astype(jnp.bfloat16)
    dquery = jnp.einsum(
        "nhqk,nkhd->nqhd", dscore_b, keys_in, preferred_element_type=jnp.float32
    ).astype(jnp.bfloat16)
    dkey = jnp.einsum(
        "nhqk,nqhd->nkhd", dscore_b, queries, preferred_element_type=jnp.float32
    ).astype(jnp.bfloat16)
    dvalue = jnp.einsum(
        "nhqk,nqhd->nkhd", rounded, dattended, preferred_element_type=jnp.float32
    ).astype(jnp.bfloat16)
    line_rows = line_count * line_len
    dprojected = jnp.concatenate(
        [
            dquery.reshape(line_rows, width),
            dkey.reshape(line_rows, width),
            dvalue.reshape(line_rows, width),
        ],
        axis=1,
    )
    home_dprojected = unpack(
        lax.all_to_all(
            scatter_lines(dprojected, places), "space", split_axis=0, concat_axis=0, tiled=True
        )
    )
    grad_qkv = contract_rows(normed, home_dprojected)
    dnormed = times_transpose(home_dprojected, w_qkv).astype(jnp.bfloat16)
    dflat_norm, grad_gain_attn = norm_back(flat, gain_attn, dnormed.astype(jnp.float32))
    grad_states = (dhidden + dflat_norm).astype(jnp.bfloat16)
    grad_qkv, grad_out, grad_gain_attn, grad_up, grad_down, grad_gain_mlp = lax.psum(
        (grad_qkv, grad_out, grad_gain_attn, grad_up, grad_down, grad_gain_mlp), ("space", "dp")
    )
    factor = 1.0 / math.sqrt(total_rows)
    return (
        output[None],
        grad_states[None],
        grad_gain_attn * factor,
        grad_qkv * factor,
        grad_out * factor,
        grad_gain_mlp * factor,
        grad_up * factor,
        grad_down * factor,
    )


def solution(mesh):
    placed = (
        P("dp", "space", None),
        P("dp", "space", None),
        P("space"),
        P("space"),
        P(),
        P(),
        P(),
        P(),
        P(),
        P(),
    )
    return jax.shard_map(
        per_device,
        mesh=mesh,
        in_specs=placed,
        out_specs=(P("dp", "space", None), P("dp", "space", None), P(), P(), P(), P(), P(), P()),
        check_vma=False,
    )
```

profile of v0, /device:TPU:1, one launch (start us, length us, event | category | flops | bytes accessed | tf_op | source)
XLA Modules:
  0.0 730.2 jit_solution(16719368341501400406)
XLA Ops:
  11.3 12.0 %all-to-all-start = ((s32[64,3,1]{1,2,0:T(1,128)}), s32[64,3,1]{1,2,0:T(1,128)S(1)}, u32[]{:S(2)}, u32[]{:S(2)}) async-start(s32[64,3,1]{1,2,0:T(1,128)} %bitcast.1), calls=%async_computation | async-start | bytes 65536 | tf_op jit(solution)/shard_map/all_to_all | solution.py:92
  32.1 6.5 scatter_custom_fusion.1
  38.6 8.2 %all_to_all.42 = bf16[64,3,12288]{2,1,0:T(4,128)(2,1)} reshape(bf16[192,12288]{1,0:T(8,128)(2,1)} %scatter_custom_fusion.1) | data formatting | bytes 9437184 | tf_op jit(solution)/shard_map/all_to_all | solution.py:91
  46.8 10.2 %all-to-all-start.1 = ((bf16[64,3,12288]{2,1,0:T(4,128)(2,1)}), bf16[64,3,12288]{2,1,0:T(4,128)(2,1)}, u32[]{:S(2)}, u32[]{:S(2)}) async-start(bf16[64,3,12288]{2,1,0:T(4,128)(2,1)} %all_to_all.42), calls=%async_computation.1 | async-start | bytes 12582912 | tf_op jit(solution)/shard_map/all_to_all | solution.py:91
  58.5 77.7 %all-to-all-done.1 = bf16[64,3,12288]{2,1,0:T(4,128)(2,1)} async-done(((bf16[64,3,12288]{2,1,0:T(4,128)(2,1)}), bf16[64,3,12288]{2,1,0:T(4,128)(2,1)}, u32[]{:S(2)}, u32[]{:S(2)}) %all-to-all-start.1) | async-done | bytes 4718624 | tf_op jit(solution)/shard_map/all_to_all | solution.py:91
  136.2 8.8 %reshape.255 = bf16[192,12288]{1,0:T(8,128)(2,1)} reshape(bf16[64,3,12288]{2,1,0:T(4,128)(2,1)} %all-to-all-done.1) | data formatting | bytes 9437184 | tf_op jit(solution)/shard_map/all_to_all | solution.py:91
  145.0 11.5 %scatter_custom_fusion.2 = bf16[192,12288]{1,0:T(8,128)(2,1)} fusion(s32[192]{0:T(256)S(1)} %bitcast.95, bf16[192,12288]{1,0:T(8,128)(2,1)} %reshape.255, bf16[]{:T(256)} %constant.29.clone.1), kind=kCustom, calls=%fused_computation.47 | custom fusion | bytes 4719104 | tf_op jit(solution)/shard_map/scatter | solution.py:81
  156.5 7.8 %reshape.191 = bf16[1536,1536]{1,0:T(8,128)(2,1)} reshape(bf16[192,12288]{1,0:T(8,128)(2,1)} %scatter_custom_fusion.2) | data formatting | bytes 9437184 | tf_op jit(solution)/shard_map/reshape | solution.py:82
  214.4 10.5 %all-to-all-start.2 = ((bf16[64,3,4096]{2,1,0:T(4,128)(2,1)}), bf16[64,3,4096]{2,1,0:T(4,128)(2,1)}, u32[]{:S(2)}, u32[]{:S(2)}) async-start(bf16[64,3,4096]{2,1,0:T(4,128)(2,1)} %broadcast_select_fusion.1), calls=%async_computation.2 | async-start | bytes 4194304 | tf_op jit(solution)/shard_map/all_to_all | solution.py:105
  226.0 26.3 %all-to-all-done.2 = bf16[64,3,4096]{2,1,0:T(4,128)(2,1)} async-done(((bf16[64,3,4096]{2,1,0:T(4,128)(2,1)}), bf16[64,3,4096]{2,1,0:T(4,128)(2,1)}, u32[]{:S(2)}, u32[]{:S(2)}) %all-to-all-start.2) | async-done | bytes 1572896 | tf_op jit(solution)/shard_map/all_to_all | solution.py:105
  276.9 33.3 %all_to_all.57 = bf16[64,3,4096]{2,1,0:T(4,128)(2,1)} all-to-all(bf16[64,3,4096]{2,1,0:T(4,128)(2,1)S(1)} %all_to_all.47), channel_id=1, replica_groups=mesh['space'=64,'dp'=2] {'space'}, dimensions={0} | all-to-all | bytes 3145728 | tf_op jit(solution)/shard_map/all_to_all | solution.py:127
  322.9 7.3 fusion.21
  330.2 14.3 %convert_bitcast_fusion.2 = bf16[48,32,8,64]{3,1,2,0:T(8,128)(2,1)} fusion(f32[48,8,32,32]{2,3,1,0:T(8,128)} %fusion.21, bf16[48,32,8,64]{3,2,1,0:T(8,128)(2,1)} %reshape.194, f32[48,8,32,32]{2,3,1,0:T(8,128)} %copy-done.5, f32[48,8,32]{2,1,0:T(8,128)S(1)} %get-tuple-element.45), kind=kOutput, calls=%fused_computation.30 | convolution fusion | flops 54669344 | bytes 6340608 | tf_op jit(solution)/shard_map/nhqk,nkhd->nqhd/dot_general | solution.py:132
  344.5 13.0 %convert_bitcast_fusion.1 = bf16[48,32,8,64]{3,1,2,0:T(8,128)(2,1)} fusion(bf16[48,32,8,64]{3,2,1,0:T(8,128)(2,1)} %reshape.193, f32[48,8,32,32]{2,3,1,0:T(8,128)} %fusion.21, f32[48,8,32,32]{2,3,1,0:T(8,128)} %copy-done.5, f32[48,8,32]{2,1,0:T(8,128)S(1)} %get-tuple-element.45), kind=kOutput, calls=%fused_computation.29 | convolution fusion | flops 54669344 | bytes 6340608 | tf_op jit(solution)/shard_map/nhqk,nqhd->nkhd/dot_general | solution.py:135
  357.5 7.1 convert_bitcast_fusion
  397.0 7.8 %reshape.201 = bf16[192,12288]{1,0:T(8,128)(2,1)} reshape(bf16[1536,1536]{1,0:T(8,128)(2,1)} %pad_maximum_fusion) | data formatting | bytes 9437184 | tf_op jit(solution)/shard_map/reshape | solution.py:85
  404.8 12.8 %gather_fusion.2 = bf16[192,12288]{1,0:T(8,128)(2,1)} fusion(bf16[192,12288]{1,0:T(8,128)(2,1)} %reshape.201, s32[1024]{0:T(1024)S(1)} %pad_clamp_fusion.1), kind=kCustom, calls=%fused_computation.2 | custom fusion | bytes 9437952 | tf_op jit(solution)/shard_map/jit(_take)/gather | solution.py:85
  417.6 8.4 %gather.22 = bf16[64,3,12288]{2,1,0:T(4,128)(2,1)} reshape(bf16[192,12288]{1,0:T(8,128)(2,1)} %gather_fusion.2) | data formatting | bytes 9437184 | tf_op jit(solution)/shard_map/jit(_take)/gather | solution.py:85
  426.0 8.1 %broadcast_select_fusion = bf16[64,3,12288]{2,1,0:T(4,128)(2,1)} fusion(bf16[64,3,12288]{2,1,0:T(4,128)(2,1)} %gather.22, pred[64,3]{1,0:T(8,128)(4,1)S(1)} %compare_and_fusion), kind=kLoop, calls=%fused_computation.14 | loop fusion | flops 2359296 | bytes 9437376 | tf_op jit(solution)/shard_map/jit(_take)/select_n | solution.py:85
  450.4 68.2 %all-to-all-done.4 = bf16[64,3,12288]{2,1,0:T(4,128)(2,1)} async-done(((bf16[64,3,12288]{2,1,0:T(4,128)(2,1)}), bf16[64,3,12288]{2,1,0:T(4,128)(2,1)}, u32[]{:S(2)}, u32[]{:S(2)}) %all-to-all-start.4) | async-done | bytes 4718624 | tf_op jit(solution)/shard_map/all_to_all | solution.py:151
  518.6 9.0 %all_to_all.51 = bf16[192,12288]{1,0:T(8,128)(2,1)} reshape(bf16[64,3,12288]{2,1,0:T(4,128)(2,1)} %all-to-all-done.4) | data formatting | bytes 9437184 | tf_op jit(solution)/shard_map/all_to_all | solution.py:151
  527.7 5.9 gather_fusion.3
  552.5 68.1 %all-reduce = (f32[512]{0:T(512)S(1)}, f32[512]{0:T(512)S(1)}) all-reduce(f32[512]{0:T(512)S(1)} %get-tuple-element.34, f32[512]{0:T(512)S(1)} %get-tuple-element.32), channel_id=1, replica_groups=mesh['space'=64,'dp'=2] {'space','dp'}, use_global_device_ids=true, to_apply=%region_18.19 | all-reduce | flops 1024 | bytes 8192 | tf_op jit(solution)/shard_map/psum | solution.py:159
  621.1 90.5 %all-reduce.4.cloned.1.call-done = (f32[512,1536]{1,0:T(8,128)}, f32[512,512]{1,0:T(8,128)}, f32[512,2048]{1,0:T(8,128)}, f32[2048,512]{1,0:T(8,128)}) async-done(((f32[512,1536]{1,0:T(8,128)}, f32[512,512]{1,0:T(8,128)}, f32[512,2048]{1,0:T(8,128)}, f32[2048,512]{1,0:T(8,128)}), (f32[512,1536]{1,0:T(8,128)}, f32[512,512]{1,0:T(8,128)}, f32[512,2048]{1,0:T(8,128)}, ...) | async-done | bytes 12582928 | tf_op jit(solution)/shard_map/psum | solution.py:159
  (144 shorter events, 182.1 us)
Async XLA Ops:
  7.2 255.3 %copy-start = (bf16[512,2048]{1,0:T(8,128)(2,1)S(1)}, bf16[512,2048]{1,0:T(8,128)(2,1)}, u32[]{:S(2)}) copy-start(bf16[512,2048]{1,0:T(8,128)(2,1)} %param.18) | copy-start | bytes 6291460
  11.3 35.5 %all-to-all-start = ((s32[64,3,1]{1,2,0:T(1,128)}), s32[64,3,1]{1,2,0:T(1,128)S(1)}, u32[]{:S(2)}, u32[]{:S(2)}) async-start(s32[64,3,1]{1,2,0:T(1,128)} %bitcast.1), calls=%async_computation | async-start | bytes 65536 | tf_op jit(solution)/shard_map/all_to_all | solution.py:92
  24.7 7.4 %copy-start.23 = (f32[512]{0:T(512)}, f32[512]{0:T(512)S(1)}, u32[]{:S(2)}) copy-start(f32[512]{0:T(512)S(1)} %broadcast_multiply_fusion.7) | copy-start | bytes 6148
  24.9 7.3 copy-start.27
  24.9 7.3 copy-start.25
  46.8 89.3 %all-to-all-start.1 = ((bf16[64,3,12288]{2,1,0:T(4,128)(2,1)}), bf16[64,3,12288]{2,1,0:T(4,128)(2,1)}, u32[]{:S(2)}, u32[]{:S(2)}) async-start(bf16[64,3,12288]{2,1,0:T(4,128)(2,1)} %all_to_all.42), calls=%async_computation.1 | async-start | bytes 12582912 | tf_op jit(solution)/shard_map/all_to_all | solution.py:91
  184.3 5.1 copy-start.2
  210.5 14.5 %copy-start.19 = (bf16[1,512,512]{2,1,0:T(8,128)(2,1)S(1)}, bf16[1,512,512]{2,1,0:T(8,128)(2,1)}, u32[]{:S(2)}) copy-start(bf16[1,512,512]{2,1,0:T(8,128)(2,1)} %param.11) | copy-start | bytes 1572868
  214.4 37.8 %all-to-all-start.2 = ((bf16[64,3,4096]{2,1,0:T(4,128)(2,1)}), bf16[64,3,4096]{2,1,0:T(4,128)(2,1)}, u32[]{:S(2)}, u32[]{:S(2)}) async-start(bf16[64,3,4096]{2,1,0:T(4,128)(2,1)} %broadcast_select_fusion.1), calls=%async_computation.2 | async-start | bytes 4194304 | tf_op jit(solution)/shard_map/all_to_all | solution.py:105
  256.5 6.0 copy-start.22
  357.5 7.1 copy-start.14
  434.1 5.9 copy-start.7
  434.1 5.9 copy-start.16
  434.1 84.5 %all-to-all-start.4 = ((bf16[64,3,12288]{2,1,0:T(4,128)(2,1)}), bf16[64,3,12288]{2,1,0:T(4,128)(2,1)}, u32[]{:S(2)}, u32[]{:S(2)}) async-start(bf16[64,3,12288]{2,1,0:T(4,128)(2,1)} %broadcast_select_fusion), calls=%async_computation.4 | async-start | bytes 12582912 | tf_op jit(solution)/shard_map/all_to_all | solution.py:151
  439.9 6.7 copy-start.21
  439.9 271.7 %all-reduce.4.cloned.1.call-start = ((), (), s32[]{:S(2)}) async-start(), calls=%async_computation.5 | async-start | bytes 25165824 | tf_op jit(solution)/shard_map/psum | solution.py:159
  440.0 6.6 copy-start.11
  527.7 7.6 %copy-start.24 = (f32[512]{0:T(512)S(1)}, f32[512]{0:T(512)}, u32[]{:S(2)}) copy-start(f32[512]{0:T(512)} %copy-done.23) | copy-start | bytes 6148
  527.7 7.6 %copy-start.26 = (f32[512]{0:T(512)S(1)}, f32[512]{0:T(512)}, u32[]{:S(2)}) copy-start(f32[512]{0:T(512)} %copy-done.25) | copy-start | bytes 6148
  527.7 7.6 %copy-start.29 = (f32[512]{0:T(512)S(1)}, f32[512]{0:T(512)}, u32[]{:S(2)}) copy-start(f32[512]{0:T(512)} %param.14) | copy-start | bytes 6148
  544.2 4.0 copy-start.28
  544.2 4.6 copy-start.4
  544.2 4.6 copy-start.9
  711.6 4.9 copy-start.12
  (12 other events, 28.3 us)
Sparse Core Ops, SparseCore 0:
  539.5 172.0 all-reduce.3
where the time goes:
time: 740 us; the launch traced here: 730 us
  waiting for transfers between devices  263 us (36%)
  local copies, waits for them, and re-layouts  196 us (26%)
  blocking collectives  101 us (14%)
  matrix products  82.9 us (11%)
  starting transfers between devices  38.5 us (5%)
  other arithmetic  33.5 us (5%)
  between operations  15 us (2%)
    psum x1, waiting for transfers between devices, per_device(): lax.psum((grad_qkv, grad_out, grad_gain_attn, grad_up, grad_down, grad_ga...  90.5 us
    all_to_all x1, waiting for transfers between devices, per_device(): lax.all_to_all(pack(home_projected), 'space', split_axis=0, concat_axis=0...  77.7 us
    all_to_all x1, waiting for transfers between devices, per_device(): lax.all_to_all(scatter_lines(dprojected, places), 'space', split_axis=0,...  68.2 us
    psum x1, blocking collectives, per_device(): lax.psum((grad_qkv, grad_out, grad_gain_attn, grad_up, grad_down, grad_ga...  68.1 us
    all_to_all x1, blocking collectives, per_device(): lax.all_to_all(pack(dmixed), 'space', split_axis=0, concat_axis=0, tiled=...  33.3 us
    gather x4, local copies, waits for them, and re-layouts, scatter_lines(): jnp.take(line_rows.reshape(slots, -1), places, axis=0, mode='fill', fill_...  31.3 us
    all_to_all x1, waiting for transfers between devices, per_device(): lax.all_to_all(scatter_lines(attended, places), 'space', split_axis=0, co...  26.3 us
    all_to_all x2, local copies, waits for them, and re-layouts, per_device(): lax.all_to_all(pack(home_projected), 'space', split_axis=0, concat_axis=0...  17 us
  transfers between devices with their start and end apart: 5, of which 4 were waited for; matrix products, arithmetic and copies ran while one was open for 6% of the time, Pallas kernels for 0%

commit v1 on v0

v1 whole, which is shorter than its diff:
```python
import math

import jax
import jax.numpy as jnp
from jax import lax
from jax.sharding import PartitionSpec as P

HEADS = 8
SEG = 8
FRAG = 4
BINS = 16
PAIRS = 4
CAP = 6

EPSILON = 1e-05
F32 = jnp.float32
BF16 = jnp.bfloat16


def dot(a, b, dims):
    return lax.dot_general(a, b, (dims, ((), ())), preferred_element_type=F32)


NN = ((1,), (0,))
NT = ((1,), (1,))
TN = ((0,), (0,))


def norm_stats(v):
    center = v - jnp.mean(v, axis=-1, keepdims=True)
    inv = lax.rsqrt(jnp.mean(center * center, axis=-1, keepdims=True) + EPSILON)
    return center * inv, inv


def norm_back(unit, inv, gain, upstream):
    g = upstream * gain
    m1 = jnp.mean(g, axis=-1, keepdims=True)
    m2 = jnp.mean(g * unit, axis=-1, keepdims=True)
    return inv * (g - m1 - unit * m2)


GELU_C = math.sqrt(2.0 / math.pi)


def gelu_parts(v):
    t = jnp.tanh(GELU_C * (v + 0.044715 * (v * v * v)))
    value = 0.5 * v * (1.0 + t)
    slope = 0.5 * (1.0 + t) + 0.5 * v * (1.0 - t * t) * (GELU_C * (1.0 + 3 * 0.044715 * (v * v)))
    return value, slope


def routing(owner, place, cap):
    n = owner.shape[0]
    ids = jnp.arange(n, dtype=jnp.int32)
    same = owner[:, None] == owner[None, :]
    rank = jnp.sum(same & (ids[None, :] < ids[:, None]), axis=1, dtype=jnp.int32)
    load = jnp.sum(same, axis=1, dtype=jnp.int32)
    first = rank == 0
    ahead = first[None, :] & (load[None, :] == load[:, None]) & (owner[None, :] < owner[:, None])
    index = jnp.sum(ahead, axis=1, dtype=jnp.int32)
    n3 = jnp.sum(first & (load == 3), dtype=jnp.int32)
    n2 = jnp.sum(first & (load == 2), dtype=jnp.int32)
    odd = (n3 % 2) == 1
    base3 = 3 * index
    base2 = 3 * n3 + 2 * index + jnp.where(odd & (index >= 1), 1, 0)
    base1 = 3 * n3 + 2 * n2 + jnp.where(odd & (n2 >= 2), 1, 0) + index
    base = jnp.where(load == 3, base3, jnp.where(load == 2, base2, base1))
    return base + rank, (base % cap) * n + place


def exchange(x):
    return lax.all_to_all(x, "space", split_axis=0, concat_axis=0, tiled=True)


def per_device(
    states, cotangent, send_owner, line_place, gain_attn, w_qkv, w_out, gain_mlp, w_up, w_down
):
    width = states.shape[2]
    rows = states.shape[1]
    nspace = lax.axis_size("space")
    total_rows = rows * nspace * lax.axis_size("dp")
    nblocks = send_owner.shape[0]
    cap = CAP
    slots = BINS * cap
    wide = 2 * (width // HEADS)
    head_dim = width // HEADS
    scale = head_dim ** (-0.5)
    slot, tag = routing(send_owner, line_place, cap)
    tags = jnp.sum(
        jnp.where(slot[None, :] == jnp.arange(slots, dtype=jnp.int32)[:, None], tag[None, :] + 1, 0), axis=1
    ) - 1
    tags = jnp.broadcast_to(tags.reshape(BINS, 1, cap), (BINS, PAIRS, cap)).reshape(nspace, cap)
    tags = exchange(tags).reshape(nspace * cap)
    nsorted = cap * nspace
    sorter = (jnp.arange(nsorted, dtype=jnp.int32)[:, None] == tags[None, :]).astype(BF16)
    target = (slot[:, None] * SEG + jnp.arange(SEG, dtype=jnp.int32)[None, :]).reshape(rows)
    pack = (jnp.arange(slots * SEG, dtype=jnp.int32)[:, None] == target[None, :]).astype(BF16)

    def to_lines(x, columns):
        x = x.reshape(BINS, cap * SEG, columns // wide // PAIRS, PAIRS, wide)
        x = x.transpose(0, 3, 1, 2, 4).reshape(nspace, cap * SEG, columns // PAIRS)
        got = exchange(x).reshape(nspace * cap, SEG * (columns // PAIRS))
        got = dot(sorter, got, NN).astype(BF16)
        return got.reshape(nsorted // FRAG, FRAG * SEG, columns // PAIRS)

    def from_lines(x):
        columns = x.shape[-1]
        back = dot(sorter, x.reshape(nsorted, SEG * columns), TN).astype(BF16)
        back = exchange(back.reshape(nspace, cap * SEG, columns))
        back = back.reshape(BINS, PAIRS, cap * SEG, columns // wide, wide).transpose(0, 2, 3, 1, 4)
        return back.reshape(slots * SEG, columns * PAIRS)

    flat_b = dot(pack, states[0], NN).astype(BF16)
    upstream = dot(pack, cotangent[0], NN).astype(BF16)
    flat = flat_b.astype(F32)
    unit_a, inv_a = norm_stats(flat)
    normed = (unit_a * gain_attn).astype(BF16)
    projected = dot(normed, w_qkv, NN).astype(BF16)
    lines = to_lines(projected, 3 * width)
    heads = (lines.shape[0], FRAG * SEG, 2, head_dim)
    queries = lines[..., :wide].reshape(heads)
    keys_in = lines[..., wide : 2 * wide].reshape(heads)
    values_in = lines[..., 2 * wide :].reshape(heads)
    expo = jnp.exp(jnp.einsum("nqhd,nkhd->nhqk", queries, keys_in, preferred_element_type=F32) * scale)
    probs = expo / jnp.sum(expo, axis=-1, keepdims=True)
    rounded = probs.astype(BF16)
    attended = jnp.einsum("nhqk,nkhd->nqhd", rounded, values_in, preferred_element_type=F32)
    attended = attended.astype(BF16).reshape(lines.shape[0], FRAG * SEG, wide)
    mixed = from_lines(attended)

    hidden = (flat + dot(mixed, w_out, NN)).astype(BF16)
    hidden32 = hidden.astype(F32)
    unit_m, inv_m = norm_stats(hidden32)
    normed_mlp = (unit_m * gain_mlp).astype(BF16)
    act32, slope = gelu_parts(dot(normed_mlp, w_up, NN))
    activated = act32.astype(BF16)
    output = (hidden32 + dot(activated, w_down, NN)).astype(BF16)
    dpre = (slope * dot(upstream, w_down, NT)).astype(BF16)
    dnormed_mlp = dot(dpre, w_up, NT)
    grad_gain_mlp = jnp.sum(unit_m * dnormed_mlp, axis=0)
    dhidden = upstream.astype(F32) + norm_back(unit_m, inv_m, gain_mlp, dnormed_mlp)
    dhidden_b = dhidden.astype(BF16)
    dmixed = dot(dhidden_b, w_out, NT).astype(BF16)
    grad_down = dot(activated, upstream, TN).astype(BF16)
    grad_up = dot(normed_mlp, dpre, TN).astype(BF16)
    grad_out = dot(mixed, dhidden_b, TN).astype(BF16)
    grad_down, grad_up, grad_out = lax.psum((grad_down, grad_up, grad_out), ("space", "dp"))

    dattended = to_lines(dmixed, width).reshape(heads)
    dprob = jnp.einsum("nqhd,nkhd->nhqk", dattended, values_in, preferred_element_type=F32)
    dscore = probs * (dprob - jnp.sum(dprob * probs, axis=-1, keepdims=True))
    dscore = (dscore * scale).astype(BF16)
    dquery = jnp.einsum("nhqk,nkhd->nqhd", dscore, keys_in, preferred_element_type=F32)
    dkey = jnp.einsum("nhqk,nqhd->nkhd", dscore, queries, preferred_element_type=F32)
    dvalue = jnp.einsum("nhqk,nqhd->nkhd", rounded, dattended, preferred_element_type=F32)
    parts = [v.astype(BF16).reshape(lines.shape[0], FRAG * SEG, wide) for v in (dquery, dkey, dvalue)]
    dprojected = from_lines(jnp.concatenate(parts, axis=-1))
    grad_qkv = dot(normed, dprojected, TN).astype(BF16)
    dnormed = dot(dprojected, w_qkv, NT).astype(BF16).astype(F32)
    grad_gain_attn = jnp.sum(unit_a * dnormed, axis=0)
    grad_states = (dhidden + norm_back(unit_a, inv_a, gain_attn, dnormed)).astype(BF16)
    output = dot(pack, output, TN).astype(BF16)
    grad_states = dot(pack, grad_states, TN).astype(BF16)
    grad_qkv, grad_gains = lax.psum((grad_qkv, jnp.stack([grad_gain_attn, grad_gain_mlp])), ("space", "dp"))
    factor = 1.0 / math.sqrt(total_rows)
    return (
        output[None],
        grad_states[None],
        grad_gains[0] * factor,
        grad_qkv.astype(F32) * factor,
        grad_out.astype(F32) * factor,
        grad_gains[1] * factor,
        grad_up.astype(F32) * factor,
        grad_down.astype(F32) * factor,
    )


def solution(mesh):
    placed = (
        P("dp", "space", None),
        P("dp", "space", None),
        P("space"),
        P("space"),
        P(),
        P(),
        P(),
        P(),
        P(),
        P(),
    )
    return jax.shard_map(
        per_device,
        mesh=mesh,
        in_specs=placed,
        out_specs=(P("dp", "space", None), P("dp", "space", None), P(), P(), P(), P(), P(), P()),
        check_vma=False,
    )
```

time: 740 us -> 495 us (0.67)
  waiting for transfers between devices: 263 us -> 134 us
  local copies, waits for them, and re-layouts: 196 us -> 107 us
  blocking collectives: 101 us -> 84.7 us
  other arithmetic: 33.5 us -> 18.7 us
    all_to_all x4, waiting for transfers between devices: 172 us -> 60.4 us  [exchange(): return lax.all_to_all(x, 'space', split_axis=0, concat_axis=0, tiled=True)]
    gather x6 -> x0, local copies, waits for them, and re-layouts: 40.2 us -> none  [the longest x4 31.3 us: scatter_lines(): jnp.take(line_rows.reshape(slots, -1), places, axis=0, mode='fill', fill_...]
    all_to_all x9 -> x1, local copies, waits for them, and re-layouts: 39.2 us -> 0.51 us  [exchange(): return lax.all_to_all(x, 'space', split_axis=0, concat_axis=0, tiled=True)]
    scatter x5 -> x0, local copies, waits for them, and re-layouts: 25.6 us -> none  [the longest x2 15.5 us: gather_lines(): jnp.zeros(received.shape, received.dtype).at[places]]
    psum x1, waiting for transfers between devices: 90.5 us -> 73.2 us  [per_device(): lax.psum((grad_qkv, jnp.stack([grad_gain_attn, grad_gain_mlp])), ('space'...]
    dot_general x15 -> x22, matrix products: 66.6 us -> 82.1 us  [the longest x19 62.7 us: dot(): return lax.dot_general(a, b, (dims, ((), ())), preferred_element_type=F32)]
    all_to_all x1, blocking collectives: 33.3 us -> 17.8 us  [exchange(): return lax.all_to_all(x, 'space', split_axis=0, concat_axis=0, tiled=True)]
    select_n x4 -> x0, other arithmetic: 12.7 us -> none  [the longest x3 12.1 us: scatter_lines(): jnp.take(line_rows.reshape(slots, -1), places, axis=0, mode='fill', fill_...]
  transfers between devices with their start and end apart: 5 -> 5, of which waited for: 4 -> 4; matrix products, arithmetic and copies ran while one was open for 6% -> 11% of each run, Pallas kernels for 0% -> 0%
where the time goes in v1:
time: 495 us; the launch traced here: 487 us
  waiting for transfers between devices  134 us (27%)
  local copies, waits for them, and re-layouts  107 us (22%)
  matrix products  89.6 us (18%)
  blocking collectives  84.7 us (17%)
  starting transfers between devices  34.4 us (7%)
  between operations  18.8 us (4%)
  other arithmetic  18.7 us (4%)
    psum x1, waiting for transfers between devices, per_device(): lax.psum((grad_qkv, jnp.stack([grad_gain_attn, grad_gain_mlp])), ('space'...  73.2 us
    psum x1, blocking collectives, per_device(): lax.psum((grad_qkv, jnp.stack([grad_gain_attn, grad_gain_mlp])), ('space'...  66.9 us
    dot_general x19, matrix products, dot(): return lax.dot_general(a, b, (dims, ((), ())), preferred_element_type=F32)  62.7 us
    all_to_all x4, waiting for transfers between devices, exchange(): return lax.all_to_all(x, 'space', split_axis=0, concat_axis=0, tiled=True)  60.4 us
    all_to_all x4, starting transfers between devices, exchange(): return lax.all_to_all(x, 'space', split_axis=0, concat_axis=0, tiled=True)  34.4 us
    all_to_all x1, blocking collectives, exchange(): return lax.all_to_all(x, 'space', split_axis=0, concat_axis=0, tiled=True)  17.8 us
    reshape x4, local copies, waits for them, and re-layouts, to_lines(): x = x.reshape(BINS, cap * SEG, columns // wide // PAIRS, PAIRS, wide)  12.1 us
  transfers between devices with their start and end apart: 5, of which 4 were waited for; matrix products, arithmetic and copies ran while one was open for 11% of the time, Pallas kernels for 0%

profile of v1, /device:TPU:1, one launch (start us, length us, event | category | flops | bytes accessed | tf_op | source)
XLA Modules:
  0.0 487.0 jit_solution(2702176918248998742)
XLA Ops:
  15.2 12.0 %all-to-all-start = ((s32[64,1,6]{2,1,0:T(1,128)}), s32[64,1,6]{2,1,0:T(1,128)S(1)}, u32[]{:S(2)}, u32[]{:S(2)}) async-start(s32[64,1,6]{2,1,0:T(1,128)} %bitcast.1), calls=%async_computation | async-start | bytes 65536 | tf_op jit(solution)/shard_map/all_to_all | solution.py:72
  33.0 5.2 %reshape.201 = bf16[16,48,3,4,128]{4,3,2,1,0:T(4,128)(2,1)} reshape(bf16[768,1536]{1,0:T(8,128)(2,1)} %convolution_convert_fusion.2) | data formatting | bytes 4718592 | tf_op jit(solution)/shard_map/reshape | solution.py:100
  38.2 5.0 %copy.139 = bf16[16,48,3,4,128]{4,2,1,3,0:T(4,128)(2,1)} copy(bf16[16,48,3,4,128]{4,3,2,1,0:T(4,128)(2,1)} %reshape.201) | data formatting | bytes 4718592 | tf_op jit(solution)/shard_map/reshape | solution.py:100
  43.2 7.1 %reshape.202 = bf16[64,48,384]{2,1,0:T(8,128)(2,1)} reshape(bf16[16,4,48,3,128]{4,3,2,1,0:T(4,128)(2,1)} %bitcast.75) | data formatting | bytes 4718592 | tf_op jit(solution)/shard_map/reshape | solution.py:101
  50.3 10.2 %all-to-all-start.1 = ((bf16[64,48,384]{2,1,0:T(8,128)(2,1)}), bf16[64,48,384]{2,1,0:T(8,128)(2,1)}, u32[]{:S(2)}, u32[]{:S(2)}) async-start(bf16[64,48,384]{2,1,0:T(8,128)(2,1)} %reshape.202), calls=%async_computation.1 | async-start | bytes 4718592 | tf_op jit(solution)/shard_map/all_to_all | solution.py:72
  62.0 29.1 %all-to-all-done.1 = bf16[64,48,384]{2,1,0:T(8,128)(2,1)} async-done(((bf16[64,48,384]{2,1,0:T(8,128)(2,1)}), bf16[64,48,384]{2,1,0:T(8,128)(2,1)}, u32[]{:S(2)}, u32[]{:S(2)}) %all-to-all-start.1) | async-done | bytes 2359328 | tf_op jit(solution)/shard_map/all_to_all | solution.py:72
  91.1 4.9 %reshape.203 = bf16[384,3072]{1,0:T(8,128)(2,1)} reshape(bf16[64,48,384]{2,1,0:T(8,128)(2,1)} %all-to-all-done.1) | data formatting | bytes 4718592 | tf_op jit(solution)/shard_map/reshape | solution.py:102
  130.6 5.2 %reshape_reshape.6 = bf16[384,1024]{1,0:T(8,128)(2,1)} reshape(bf16[96,32,2,64]{3,2,1,0:T(2,128)(2,1)} %copy.100) | data formatting | bytes 1572864 | tf_op jit(solution)/shard_map/reshape;reshape | solution.py:108
  138.8 6.3 %all-to-all-start.2 = ((bf16[64,48,128]{2,1,0:T(8,128)(2,1)}), bf16[64,48,128]{2,1,0:T(8,128)(2,1)S(1)}, u32[]{:S(2)}, u32[]{:S(2)}) async-start(bf16[64,48,128]{2,1,0:T(8,128)(2,1)} %reshape.208), calls=%async_computation.2 | async-start | bytes 1572864 | tf_op jit(solution)/shard_map/all_to_all | solution.py:72
  147.7 11.7 %all-to-all-done.2 = bf16[64,48,128]{2,1,0:T(8,128)(2,1)S(1)} async-done(((bf16[64,48,128]{2,1,0:T(8,128)(2,1)}), bf16[64,48,128]{2,1,0:T(8,128)(2,1)S(1)}, u32[]{:S(2)}, u32[]{:S(2)}) %all-to-all-start.2) | async-done | bytes 786464 | tf_op jit(solution)/shard_map/all_to_all | solution.py:72
  164.7 5.0 %fusion.10 = bf16[768,2048]{1,0:T(8,128)(2,1)S(1)} fusion(f32[768,2048]{1,0:T(8,128)S(1)} %fusion.107, bf16[768,512]{0,1:T(8,128)(2,1)S(1)} %copy-done.17, bf16[2048,512]{1,0:T(8,128)(2,1)S(1)} %copy-done.21), kind=kOutput, calls=%fused_computation.12 | convolution fusion | flops 1638924288 | bytes 12320768 | tf_op jit(solution)/shard_map/dot_general | solution.py:21
  175.8 17.8 %all_to_all.29 = bf16[64,48,128]{2,1,0:T(8,128)(2,1)S(1)} all-to-all(bf16[64,48,128]{2,1,0:T(8,128)(2,1)S(1)} %bitcast.84), channel_id=1, replica_groups=mesh['space'=64,'dp'=2] {'space'}, dimensions={0} | all-to-all | bytes 1572864 | tf_op jit(solution)/shard_map/all_to_all | solution.py:72
  205.1 8.2 %fusion.68 = bf16[96,32,2,64]{3,1,2,0:T(8,128)(2,1)} fusion(bf16[96,32,2,64]{3,1,2,0:T(8,128)(2,1)} %copy.97, f32[96,2,32,32]{2,3,1,0:T(8,128)} %fusion.74, f32[96,2,32,32]{2,3,1,0:T(8,128)} %copy-done.4, f32[96,2,32]{2,1,0:T(2,128)S(1)} %get-tuple-element.33), kind=kOutput, calls=%fused_computation.84 | convolution fusion | flops 27334688 | bytes 3170304 | tf_op jit(solution)/shard_map/nhqk,nkhd->nqhd/dot_general | solution.py:153
  213.3 8.1 %fusion.65 = bf16[96,32,2,64]{3,1,2,0:T(8,128)(2,1)} fusion(bf16[96,32,2,64]{3,1,2,0:T(8,128)(2,1)} %copy.96, f32[96,2,32,32]{2,3,1,0:T(8,128)} %fusion.74, f32[96,2,32,32]{2,3,1,0:T(8,128)} %copy-done.4, f32[96,2,32]{2,1,0:T(2,128)S(1)} %get-tuple-element.33), kind=kOutput, calls=%fused_computation.83 | convolution fusion | flops 27334688 | bytes 3170304 | tf_op jit(solution)/shard_map/nhqk,nqhd->nkhd/dot_general | solution.py:154
  253.3 5.9 %all-to-all-start.4 = ((bf16[64,48,384]{2,1,0:T(8,128)(2,1)}), bf16[64,48,384]{2,1,0:T(8,128)(2,1)}, u32[]{:S(2)}, u32[]{:S(2)}) async-start(bf16[64,48,384]{2,1,0:T(8,128)(2,1)} %reshape.218), calls=%async_computation.4 | async-start | bytes 4718592 | tf_op jit(solution)/shard_map/all_to_all | solution.py:72
  260.7 5.3 %convolution_convert_fusion.4 = bf16[512,2048]{1,0:T(8,128)(2,1)} fusion(bf16[768,2048]{1,0:T(8,128)(2,1)} %copy-done.25, bf16[768,512]{0,1:T(8,128)(2,1)S(1)} %copy-done.9, f32[512]{0:T(512)S(1)} %copy-done.20, f32[768]{0:T(1024)S(1)} %add_rsqrt_fusion, f32[768]{0:T(1024)S(1)} %broadcast_multiply_fusion.4), kind=kOutput, calls=%fused_computation.27 | convolution fusion | flops 1613627392 | bytes 6037504 | tf_op jit(solution)/shard_map/dot_general | solution.py:21
  269.7 19.6 %all-to-all-done.4 = bf16[64,48,384]{2,1,0:T(8,128)(2,1)} async-done(((bf16[64,48,384]{2,1,0:T(8,128)(2,1)}), bf16[64,48,384]{2,1,0:T(8,128)(2,1)}, u32[]{:S(2)}, u32[]{:S(2)}) %all-to-all-start.4) | async-done | bytes 2359328 | tf_op jit(solution)/shard_map/all_to_all | solution.py:72
  289.3 7.0 %reshape.219 = bf16[16,4,48,3,128]{4,3,2,1,0:T(4,128)(2,1)} reshape(bf16[64,48,384]{2,1,0:T(8,128)(2,1)} %all-to-all-done.4) | data formatting | bytes 4718592 | tf_op jit(solution)/shard_map/reshape | solution.py:110
  296.4 6.5 %copy.115 = bf16[16,48,3,4,128]{4,3,2,1,0:T(4,128)(2,1)} copy(bf16[16,48,3,4,128]{4,2,1,3,0:T(4,128)(2,1)} %bitcast.76) | data formatting | bytes 4718592 | tf_op jit(solution)/shard_map/transpose | solution.py:110
  302.9 5.1 %reshape.220 = bf16[768,1536]{1,0:T(8,128)(2,1)} reshape(bf16[16,48,3,4,128]{4,3,2,1,0:T(4,128)(2,1)} %copy.115) | data formatting | bytes 4718592 | tf_op jit(solution)/shard_map/reshape | solution.py:111
  313.4 8.1 %fusion.76 = bf16[1,512,512]{2,1,0:T(8,128)(2,1)} fusion(s32[512]{0:T(512)S(1)} %add.163, bf16[768,512]{0,1:T(8,128)(2,1)S(1)} %copy-done.10, bf16[2048,512]{1,0:T(8,128)(2,1)} %param.19, f32[768,2048]{1,0:T(8,128)} %copy-done.24), kind=kOutput, calls=%fused_computation.98 | convolution fusion | flops 2029649920 | bytes 9701376 | tf_op jit(solution)/shard_map/dot_general | solution.py:21
  321.5 4.9 %fusion.55 = (f32[512]{0:T(512)S(1)}, f32[768]{0:T(1024)S(1)}, f32[768]{0:T(1024)S(1)}, bf16[768,512]{0,1:T(8,128)(2,1)}) fusion(bf16[768,512]{0,1:T(8,128)(2,1)} %copy-done.14, f32[768]{0:T(1024)S(1)} %add_rsqrt_fusion.1, f32[768]{0:T(1024)S(1)} %broadcast_multiply_fusion.5, f32[512]{0:T(512)S(1)} %copy-done.23, bf16[768,1536]{1,0:T(8,128)(2,1)} %reshape.220, ...), kind=kOutput, calls=%fused_computation.72 | convolution fusion | flops 1212282880 | bytes 5521408 | tf_op jit(solution)/shard_map/dot_general | solution.py:21
  326.4 66.9 %psum.35 = f32[2,512]{1,0:T(2,128)S(1)} all-reduce(f32[2,512]{1,0:T(2,128)S(1)} %pad_maximum_fusion.1), channel_id=1, replica_groups=mesh['space'=64,'dp'=2] {'space','dp'}, use_global_device_ids=true, to_apply=%region_18.19 | all-reduce | flops 1024 | bytes 8192 | tf_op jit(solution)/shard_map/psum | solution.py:164
  396.9 73.2 %all-reduce.3.cloned.1.call-done = (bf16[512,1536]{1,0:T(8,128)(2,1)}, bf16[512,512]{1,0:T(8,128)(2,1)}, bf16[512,2048]{1,0:T(8,128)(2,1)}, bf16[2048,512]{1,0:T(8,128)(2,1)}) async-done(((bf16[512,1536]{1,0:T(8,128)(2,1)}, bf16[512,512]{1,0:T(8,128)(2,1)}, bf16[512,2048]{1,0:T(8,128)(2,1)}, bf16[2048,512]{1,0:T(8,128)(2,1)}), (bf16[512,1536]{1,0:T(8,128)(2,1)}, bf16[512,512]{1,0:T(8,128)(2,1)}, ...) | async-done | bytes 6291472 | tf_op jit(solution)/shard_map/psum | solution.py:164
  (132 shorter events, 129.7 us)
Async XLA Ops:
  7.2 155.5 %copy-start = (bf16[512,2048]{1,0:T(8,128)(2,1)S(1)}, bf16[512,2048]{1,0:T(8,128)(2,1)}, u32[]{:S(2)}) copy-start(bf16[512,2048]{1,0:T(8,128)(2,1)} %param.18) | copy-start | bytes 6291460
  7.2 22.9 %copy-start.23 = (f32[512]{0:T(512)S(1)}, f32[512]{0:T(512)}, u32[]{:S(2)}) copy-start(f32[512]{0:T(512)} %param.14) | copy-start | bytes 6148
  15.2 35.1 %all-to-all-start = ((s32[64,1,6]{2,1,0:T(1,128)}), s32[64,1,6]{2,1,0:T(1,128)S(1)}, u32[]{:S(2)}, u32[]{:S(2)}) async-start(s32[64,1,6]{2,1,0:T(1,128)} %bitcast.1), calls=%async_computation | async-start | bytes 65536 | tf_op jit(solution)/shard_map/all_to_all | solution.py:72
  27.3 2.7 copy-start.22
  50.3 40.7 %all-to-all-start.1 = ((bf16[64,48,384]{2,1,0:T(8,128)(2,1)}), bf16[64,48,384]{2,1,0:T(8,128)(2,1)}, u32[]{:S(2)}, u32[]{:S(2)}) async-start(bf16[64,48,384]{2,1,0:T(8,128)(2,1)} %reshape.202), calls=%async_computation.1 | async-start | bytes 4718592 | tf_op jit(solution)/shard_map/all_to_all | solution.py:72
  123.0 3.0 copy-start.2
  138.8 21.9 %copy-start.19 = (bf16[512,512]{1,0:T(8,128)(2,1)S(1)}, bf16[512,512]{1,0:T(8,128)(2,1)}, u32[]{:S(2)}) copy-start(bf16[512,512]{1,0:T(8,128)(2,1)} %param.16) | copy-start | bytes 1572868
  138.8 20.6 %all-to-all-start.2 = ((bf16[64,48,128]{2,1,0:T(8,128)(2,1)}), bf16[64,48,128]{2,1,0:T(8,128)(2,1)S(1)}, u32[]{:S(2)}, u32[]{:S(2)}) async-start(bf16[64,48,128]{2,1,0:T(8,128)(2,1)} %reshape.208), calls=%async_computation.2 | async-start | bytes 1572864 | tf_op jit(solution)/shard_map/all_to_all | solution.py:72
  159.8 2.9 copy-start.20
  162.4 9.4 %copy-start.8 = (bf16[768,512]{0,1:T(8,128)(2,1)}, bf16[768,512]{0,1:T(8,128)(2,1)S(1)}, u32[]{:S(2)}) copy-start(bf16[768,512]{0,1:T(8,128)(2,1)S(1)} %get-tuple-element.36) | copy-start | bytes 2359300
  164.7 5.0 %copy-start.24 = (f32[768,2048]{1,0:T(8,128)}, f32[768,2048]{1,0:T(8,128)S(1)}, u32[]{:S(2)}) copy-start(f32[768,2048]{1,0:T(8,128)S(1)} %fusion.107) | copy-start | bytes 18874372
  198.4 4.6 copy-start.3
  198.4 4.6 copy-start.5
  253.3 6.0 %copy-start.7 = (bf16[16,48,1,4,128]{4,3,1,0,2:T(4,128)(2,1)S(1)}, bf16[16,48,1,4,128]{4,3,1,0,2:T(4,128)(2,1)}, u32[]{:S(2)}) copy-start(bf16[16,48,1,4,128]{4,3,1,0,2:T(4,128)(2,1)} %copy-done.6) | copy-start | bytes 2359300
  253.3 36.0 %all-to-all-start.4 = ((bf16[64,48,384]{2,1,0:T(8,128)(2,1)}), bf16[64,48,384]{2,1,0:T(8,128)(2,1)}, u32[]{:S(2)}, u32[]{:S(2)}) async-start(bf16[64,48,384]{2,1,0:T(8,128)(2,1)} %reshape.218), calls=%async_computation.4 | async-start | bytes 4718592 | tf_op jit(solution)/shard_map/all_to_all | solution.py:72
  259.2 210.9 %all-reduce.3.cloned.1.call-start = ((), (), s32[]{:S(2)}) async-start(), calls=%async_computation.5 | async-start | bytes 12582912 | tf_op jit(solution)/shard_map/psum | solution.py:164
  259.3 6.8 %slice-start = ((s8[6291456]{0:T(1024)(128)(4,1)}), s8[4194304]{0:T(1024)(128)(4,1)S(1)}, s32[]{:S(2)}) async-start(s8[6291456]{0:T(1024)(128)(4,1)} %bitcast.91), calls=%async_computation.6 | async-start | bytes 8388608
  260.7 5.3 %copy-start.18 = (bf16[768,512]{0,1:T(8,128)(2,1)S(1)}, bf16[768,512]{0,1:T(8,128)(2,1)}, u32[]{:S(2)}) copy-start(bf16[768,512]{0,1:T(8,128)(2,1)} %fusion.72) | copy-start | bytes 2359300
  260.7 5.3 %slice-start.1 = ((s8[6291456]{0:T(1024)(128)(4,1)}), s8[2097152]{0:T(1024)(128)(4,1)S(1)}, s32[]{:S(2)}) async-start(s8[6291456]{0:T(1024)(128)(4,1)} %bitcast.91), calls=%async_computation.7 | async-start | bytes 4194304
  302.9 5.1 %copy-start.15 = (bf16[768,512]{0,1:T(8,128)(2,1)S(1)}, bf16[768,512]{0,1:T(8,128)(2,1)}, u32[]{:S(2)}) copy-start(bf16[768,512]{0,1:T(8,128)(2,1)} %copy-done.14) | copy-start | bytes 2359300
  321.5 72.4 %copy-start.16 = (bf16[768,512]{0,1:T(8,128)(2,1)S(1)}, bf16[768,512]{0,1:T(8,128)(2,1)}, u32[]{:S(2)}) copy-start(bf16[768,512]{0,1:T(8,128)(2,1)} %copy-done.14) | copy-start | bytes 2359300
  470.1 2.3 copy-start.13
  474.5 2.6 copy-start.11
  477.1 2.6 copy-start.1
  (9 other events, 14.2 us)
Sparse Core Ops, SparseCore 0:
  312.4 157.6 all-reduce.2

commit v2 on v1

--- a/solution.py
+++ b/solution.py
@@ -1,8 +1,11 @@
+import functools
 import math
 
 import jax
 import jax.numpy as jnp
 from jax import lax
+from jax.experimental import pallas as pl
+from jax.experimental.pallas import tpu as pltpu
 from jax.sharding import PartitionSpec as P
 
 HEADS = 8
@@ -15,6 +18,7 @@
 EPSILON = 1e-05
 F32 = jnp.float32
 BF16 = jnp.bfloat16
+MESH = pl.DeviceIdType.MESH
 
 
 def dot(a, b, dims):
@@ -68,8 +72,261 @@
     return base + rank, (base % cap) * n + place
 
 
-def exchange(x):
-    return lax.all_to_all(x, "space", split_axis=0, concat_axis=0, tiled=True)
+def partner_of(me, k):
+    ys = lax.rem(lax.div(me, 16) + lax.div(k, 16), 4)
+    zs = lax.rem(lax.div(lax.rem(me, 16), 4) + lax.div(lax.rem(k, 16), 4), 4)
+    xs = lax.rem(lax.rem(me, 4) + lax.rem(k, 4), 4)
+    return ys * 16 + zs * 4 + xs
+
+
+def greet_all(me, count):
+    barrier = pltpu.get_barrier_semaphore()
+
+    def greet(k, carry):
+        pl.semaphore_signal(barrier, inc=1, device_id={"space": partner_of(me, k)}, device_id_type=MESH)
+        return carry
+
+    lax.fori_loop(1, count, greet, 0)
+    pl.semaphore_wait(barrier, count - 1)
+
+
+def remote(src, dst, send_sem, recv_sem, device):
+    return pltpu.make_async_remote_copy(
+        src_ref=src, dst_ref=dst, send_sem=send_sem, recv_sem=recv_sem,
+        device_id={"space": device}, device_id_type=MESH,
+    )
+
+
+def lanes(j, pair):
+    return pl.ds(pl.multiple_of(j * 512 + pair * 128, 128), 128)
+
+
+def send_to_lines(me, count, pieces, src, recv, send_sem, recv_sem, extra=None):
+    def send(k, carry):
+        to = partner_of(me, k)
+        for j in range(pieces):
+            remote(src.at[lax.div(to, PAIRS), :, lanes(j, lax.rem(to, PAIRS))],
+                   recv.at[me, :, pl.ds(128 * j, 128)], send_sem, recv_sem, to).start()
+        if extra is not None:
+            remote(extra[0].at[lax.div(to, PAIRS)], extra[1].at[me], extra[2], extra[3], to).start()
+        return carry
+
+    for j in range(pieces):
+        pltpu.make_async_copy(src.at[lax.div(me, PAIRS), :, lanes(j, lax.rem(me, PAIRS))],
+                              recv.at[me, :, pl.ds(128 * j, 128)], recv_sem).start()
+    if extra is not None:
+        pltpu.make_async_copy(extra[0].at[lax.div(me, PAIRS)], extra[1].at[me], extra[3]).start()
+    lax.fori_loop(1, count, send, 0)
+
+
+def send_home(me, count, pieces, src, home, send_sem, recv_sem):
+    mine = lax.div(me, PAIRS)
+    pair = lax.rem(me, PAIRS)
+
+    def send(k, carry):
+        to = partner_of(me, k)
+        for j in range(pieces):
+            remote(src.at[to, :, pl.ds(128 * j, 128)], home.at[mine, :, lanes(j, pair)],
+                   send_sem, recv_sem, to).start()
+        return carry
+
+    for j in range(pieces):
+        pltpu.make_async_copy(src.at[me, :, pl.ds(128 * j, 128)], home.at[mine, :, lanes(j, pair)], recv_sem).start()
+    lax.fori_loop(1, count, send, 0)
+
+
+def await_bytes(ref, sem):
+    pltpu.make_async_copy(ref, ref, sem).wait()
+
+
+def build_sorter(table, sorter):
+    n = sorter.shape[0]
+    for c in range(n // 128):
+        ids = lax.broadcasted_iota(jnp.int32, (n, 128), 0)
+        sorter[:, pl.ds(128 * c, 128)] = jnp.where(ids == table[c : c + 1, :] - 1, 1.0, 0.0).astype(BF16)
+
+
+def sort_blocks(cap, recv, wide32, gathered, sorter, out):
+    count = recv.shape[0]
+    span = cap * SEG
+
+    def widen(d, carry):
+        for j in range(wide32.shape[0]):
+            part = recv[d, :, pl.ds(128 * j, 128)]
+            wide32[j, pl.ds(pl.multiple_of(d * span, 8), span), :] = part.astype(F32)
+        return carry
+
+    lax.fori_loop(0, count, widen, 0)
+
+    for r in range(SEG):
+        for s in range(cap):
+            for j in range(wide32.shape[0]):
+                part = wide32[j, pl.ds(s * SEG + r, count, stride=span), :]
+                gathered[pl.ds(s * count, count), pl.ds(128 * j, 128)] = part.astype(BF16)
+        out[r] = dot(sorter[...], gathered[...], NN).astype(BF16)
+
+
+def unsort_blocks(cap, src, wide32, sorter, out):
+    count = out.shape[0]
+    span = cap * SEG
+    for r in range(SEG):
+        back = dot(sorter[...], src[r], TN)
+        for s in range(cap):
+            for j in range(wide32.shape[0]):
+                part = back[s * count : (s + 1) * count, 128 * j : 128 * (j + 1)]
+                wide32[j, pl.ds(s * SEG + r, count, stride=span), :] = part
+
+    def narrow(d, carry):
+        for j in range(wide32.shape[0]):
+            part = wide32[j, pl.ds(pl.multiple_of(d * span, 8), span), :]
+            out[d, :, pl.ds(128 * j, 128)] = part.astype(BF16)
+        return carry
+
+    lax.fori_loop(0, count, narrow, 0)
+
+
+TILE = 32
+
+
+def same_line():
+    n = TILE * SEG
+    a = lax.div(lax.rem(lax.broadcasted_iota(jnp.int32, (n, n), 0), TILE), FRAG)
+    b = lax.div(lax.rem(lax.broadcasted_iota(jnp.int32, (n, n), 1), TILE), FRAG)
+    return a == b
+
+
+def head_probs(q, k, first, mask, scale):
+    q = jnp.where(first, q, jnp.zeros_like(q))
+    expo = jnp.where(mask, jnp.exp(dot(q, k, NT) * scale), 0.0)
+    return expo / jnp.sum(expo, axis=-1, keepdims=True)
+
+
+def forward_kernel(cap, scale, proj, tagt, mixed, lines, table, recv, trecv, wide32, gathered, sorter,
+                   attended, wide128, back, sems):
+    me = lax.axis_index("space")
+    count = recv.shape[0]
+    greet_all(me, count)
+    send_to_lines(me, count, 3, proj, recv, sems.at[0], sems.at[1], (tagt, trecv, sems.at[2], sems.at[3]))
+    await_bytes(trecv, sems.at[3])
+    table[...] = jnp.sum(trecv[...], axis=0)
+    build_sorter(table[...], sorter)
+    await_bytes(recv, sems.at[1])
+    sort_blocks(cap, recv, wide32, gathered, sorter, lines)
+    n = TILE * SEG
+    mask = same_line()
+    low = lax.broadcasted_iota(jnp.int32, (n, 128), 1) < 64
+
+    def attend(t, carry):
+        part = pl.ds(pl.multiple_of(t * TILE, TILE), TILE)
+        x = lines[:, part, :].reshape(n, 384)
+        q, k, v = x[:, :128], x[:, 128:256], x[:, 256:]
+        outs = []
+        for first in (low, ~low):
+            w = head_probs(q, k, first, mask, scale).astype(BF16)
+            outs.append(dot(w, v, NN))
+        attended[:, part, :] = jnp.where(low, outs[0], outs[1]).astype(BF16).reshape(SEG, TILE, 128)
+        return carry
+
+    lax.fori_loop(0, cap * count // TILE, attend, 0)
+    unsort_blocks(cap, attended, wide128, sorter, back)
+    send_home(me, count, 1, back, mixed, sems.at[4], sems.at[5])
+    await_bytes(recv.at[pl.ds(0, count - 1)], sems.at[0])
+    await_bytes(trecv.at[pl.ds(0, count - 1)], sems.at[2])
+    await_bytes(back.at[pl.ds(0, count - 1)], sems.at[4])
+    await_bytes(mixed, sems.at[5])
+
+
+def backward_kernel(cap, scale, dmixed, lines, table, dproj, recv, wide128, gathered, sorter, dlines_in,
+                    dlines, wide32, back, sems):
+    me = lax.axis_index("space")
+    count = recv.shape[0]
+    greet_all(me, count)
+    send_to_lines(me, count, 1, dmixed, recv, sems.at[0], sems.at[1])
+    build_sorter(table[...], sorter)
+    await_bytes(recv, sems.at[1])
+    sort_blocks(cap, recv, wide128, gathered, sorter, dlines_in)
+    n = TILE * SEG
+    mask = same_line()
+    low = lax.broadcasted_iota(jnp.int32, (n, 128), 1) < 64
+
+    def attend(t, carry):
+        part = pl.ds(pl.multiple_of(t * TILE, TILE), TILE)
+        x = lines[:, part, :].reshape(n, 384)
+        up = dlines_in[:, part, :].reshape(n, 128)
+        q, k, v = x[:, :128], x[:, 128:256], x[:, 256:]
+        outs = []
+        for first in (low, ~low):
+            p = head_probs(q, k, first, mask, scale)
+            g = dot(jnp.where(first, up, jnp.zeros_like(up)), v, NT)
+            ds = (p * (g - jnp.sum(g * p, axis=-1, keepdims=True)) * scale).astype(BF16)
+            outs.append((dot(ds, k, NN), dot(ds, q, TN), dot(p.astype(BF16), up, TN)))
+        for j in range(3):
+            dlines[:, part, pl.ds(128 * j, 128)] = (
+                jnp.where(low, outs[0][j], outs[1][j]).astype(BF16).reshape(SEG, TILE, 128)
+            )
+        return carry
+
+    lax.fori_loop(0, cap * count // TILE, attend, 0)
+    unsort_blocks(cap, dlines, wide32, sorter, back)
+    send_home(me, count, 3, back, dproj, sems.at[2], sems.at[3])
+    await_bytes(recv.at[pl.ds(0, count - 1)], sems.at[0])
+    await_bytes(back.at[pl.ds(0, count - 1)], sems.at[2])
+    await_bytes(dproj, sems.at[3])
+
+
+VM = pl.BlockSpec(memory_space=pltpu.VMEM)
+
+
+def forward_lines(proj, tagt, cap, count, scale):
+    n = cap * count
+    span = cap * SEG
+    return pl.pallas_call(
+        functools.partial(forward_kernel, cap, scale),
+        out_shape=(
+            jax.ShapeDtypeStruct((BINS, span, 512), BF16),
+            jax.ShapeDtypeStruct((SEG, n, 384), BF16),
+            jax.ShapeDtypeStruct((8, 128), jnp.int32),
+        ),
+        in_specs=[VM] * 2,
+        out_specs=(VM,) * 3,
+        scratch_shapes=[
+            pltpu.VMEM((count, span, 384), BF16),
+            pltpu.VMEM((count, 8, 128), jnp.int32),
+            pltpu.VMEM((3, count * span, 128), F32),
+            pltpu.VMEM((n, 384), BF16),
+            pltpu.VMEM((n, n), BF16),
+            pltpu.VMEM((SEG, n, 128), BF16),
+            pltpu.VMEM((1, count * span, 128), F32),
+            pltpu.VMEM((count, span, 128), BF16),
+            pltpu.SemaphoreType.DMA((6,)),
+        ],
+        compiler_params=pltpu.CompilerParams(collective_id=1, has_side_effects=True, vmem_limit_bytes=60 << 20),
+        name="forward_lines",
+    )(proj, tagt)
+
+
+def backward_lines(dmixed, lines, table, cap, count, scale):
+    n = cap * count
+    span = cap * SEG
+    return pl.pallas_call(
+        functools.partial(backward_kernel, cap, scale),
+        out_shape=jax.ShapeDtypeStruct((BINS, span, 1536), BF16),
+        in_specs=[VM] * 3,
+        out_specs=VM,
+        scratch_shapes=[
+            pltpu.VMEM((count, span, 128), BF16),
+            pltpu.VMEM((1, count * span, 128), F32),
+            pltpu.VMEM((n, 128), BF16),
+            pltpu.VMEM((n, n), BF16),
+            pltpu.VMEM((SEG, n, 128), BF16),
+            pltpu.VMEM((SEG, n, 384), BF16),
+            pltpu.VMEM((3, count * span, 128), F32),
+            pltpu.VMEM((count, span, 384), BF16),
+            pltpu.SemaphoreType.DMA((4,)),
+        ],
+        compiler_params=pltpu.CompilerParams(collective_id=2, has_side_effects=True, vmem_limit_bytes=60 << 20),
+        name="backward_lines",
+    )(dmixed, lines, table)
 
 
 def per_device(
@@ -86,29 +343,14 @@
     head_dim = width // HEADS
     scale = head_dim ** (-0.5)
     slot, tag = routing(send_owner, line_place, cap)
-    tags = jnp.sum(
-        jnp.where(slot[None, :] == jnp.arange(slots, dtype=jnp.int32)[:, None], tag[None, :] + 1, 0), axis=1
-    ) - 1
-    tags = jnp.broadcast_to(tags.reshape(BINS, 1, cap), (BINS, PAIRS, cap)).reshape(nspace, cap)
-    tags = exchange(tags).reshape(nspace * cap)
-    nsorted = cap * nspace
-    sorter = (jnp.arange(nsorted, dtype=jnp.int32)[:, None] == tags[None, :]).astype(BF16)
+    me = lax.axis_index("space")
+    hit = slot[None, :] == jnp.arange(slots, dtype=jnp.int32)[:, None]
+    tags = jnp.sum(jnp.where(hit, tag[None, :] + 1, 0), axis=1).reshape(BINS, cap // 2, 2)
+    tags = jnp.pad(tags, ((0, 0), (0, 8 - cap // 2), (0, 0)))
+    at_me = jnp.arange(nspace, dtype=jnp.int32) == me
+    tagt = jnp.where(at_me[None, None, None, :], tags[..., None], 0).reshape(BINS, 8, 2 * nspace)
     target = (slot[:, None] * SEG + jnp.arange(SEG, dtype=jnp.int32)[None, :]).reshape(rows)
     pack = (jnp.arange(slots * SEG, dtype=jnp.int32)[:, None] == target[None, :]).astype(BF16)
-
-    def to_lines(x, columns):
-        x = x.reshape(BINS, cap * SEG, columns // wide // PAIRS, PAIRS, wide)
-        x = x.transpose(0, 3, 1, 2, 4).reshape(nspace, cap * SEG, columns // PAIRS)
-        got = exchange(x).reshape(nspace * cap, SEG * (columns // PAIRS))
-        got = dot(sorter, got, NN).astype(BF16)
-        return got.reshape(nsorted // FRAG, FRAG * SEG, columns // PAIRS)
-
-    def from_lines(x):
-        columns = x.shape[-1]
-        back = dot(sorter, x.reshape(nsorted, SEG * columns), TN).astype(BF16)
-        back = exchange(back.reshape(nspace, cap * SEG, columns))
-        back = back.reshape(BINS, PAIRS, cap * SEG, columns // wide, wide).transpose(0, 2, 3, 1, 4)
-        return back.reshape(slots * SEG, columns * PAIRS)
 
     flat_b = dot(pack, states[0], NN).astype(BF16)
     upstream = dot(pack, cotangent[0], NN).astype(BF16)
@@ -116,17 +358,9 @@
     unit_a, inv_a = norm_stats(flat)
     normed = (unit_a * gain_attn).astype(BF16)
     projected = dot(normed, w_qkv, NN).astype(BF16)
-    lines = to_lines(projected, 3 * width)
-    heads = (lines.shape[0], FRAG * SEG, 2, head_dim)
-    queries = lines[..., :wide].reshape(heads)
-    keys_in = lines[..., wide : 2 * wide].reshape(heads)
-    values_in = lines[..., 2 * wide :].reshape(heads)
-    expo = jnp.exp(jnp.einsum("nqhd,nkhd->nhqk", queries, keys_in, preferred_element_type=F32) * scale)
-    probs = expo / jnp.sum(expo, axis=-1, keepdims=True)
-    rounded = probs.astype(BF16)
-    attended = jnp.einsum("nhqk,nkhd->nqhd", rounded, values_in, preferred_element_type=F32)
-    attended = attended.astype(BF16).reshape(lines.shape[0], FRAG * SEG, wide)
-    mixed = from_lines(attended)
+    span = cap * SEG
+    mixed, lines, table = forward_lines(projected.reshape(BINS, span, 3 * width), tagt, cap, nspace, scale)
+    mixed = mixed.reshape(BINS * span, width)
 
     hidden = (flat + dot(mixed, w_out, NN)).astype(BF16)
     hidden32 = hidden.astype(F32)
@@ -146,15 +380,8 @@
     grad_out = dot(mixed, dhidden_b, TN).astype(BF16)
     grad_down, grad_up, grad_out = lax.psum((grad_down, grad_up, grad_out), ("space", "dp"))
 
-    dattended = to_lines(dmixed, width).reshape(heads)
-    dprob = jnp.einsum("nqhd,nkhd->nhqk", dattended, values_in, preferred_element_type=F32)
-    dscore = probs * (dprob - jnp.sum(dprob * probs, axis=-1, keepdims=True))
-    dscore = (dscore * scale).astype(BF16)
-    dquery = jnp.einsum("nhqk,nkhd->nqhd", dscore, keys_in, preferred_element_type=F32)
-    dkey = jnp.einsum("nhqk,nqhd->nkhd", dscore, queries, preferred_element_type=F32)
-    dvalue = jnp.einsum("nhqk,nqhd->nkhd", rounded, dattended, preferred_element_type=F32)
-    parts = [v.astype(BF16).reshape(lines.shape[0], FRAG * SEG, wide) for v in (dquery, dkey, dvalue)]
-    dprojected = from_lines(jnp.concatenate(parts, axis=-1))
+    dprojected = backward_lines(dmixed.reshape(BINS, span, width), lines, table, cap, nspace, scale)
+    dprojected = dprojected.reshape(BINS * span, 3 * width)
     grad_qkv = dot(normed, dprojected, TN).astype(BF16)
     dnormed = dot(dprojected, w_qkv, NT).astype(BF16).astype(F32)
     grad_gain_attn = jnp.sum(unit_a * dnormed, axis=0)

time: 495 us -> 373 us (0.75); the launches traced: 487 us -> 373 us
  Pallas kernels: 0 us -> 143 us
  local copies, waits for them, and re-layouts: 107 us -> 1.31 us
  waiting for transfers between devices: 134 us -> 76.3 us
  matrix products: 89.6 us -> 48.3 us
  starting transfers between devices: 34.4 us -> 0.04 us
  blocking collectives: 84.7 us -> 70.4 us
    pallas_call x0 -> x2, Pallas kernels: none -> 143 us  [the longest x1 78 us: forward_lines(): pl.pallas_call(functools.partial(forward_kernel, cap, scale), out_shape=(...]
    reshape x16 -> x1, local copies, waits for them, and re-layouts: 62.7 us -> 0.14 us  [per_device(): jnp.sum(jnp.where(hit, tag[None, :] + 1, 0), axis=1)]
    all_to_all x4 -> x0, waiting for transfers between devices: 60.4 us -> none  [exchange(): return lax.all_to_all(x, 'space', split_axis=0, concat_axis=0, tiled=True)]
    all_to_all x4 -> x0, starting transfers between devices: 34.4 us -> none  [exchange(): return lax.all_to_all(x, 'space', split_axis=0, concat_axis=0, tiled=True)]
    dot_general x6 -> x0, matrix products: 26.9 us -> none  [the longest x1 8.24 us: per_device(): jnp.einsum('nhqk,nkhd->nqhd', dscore, keys_in, preferred_element_type=F32)]
    all_to_all x1 -> x0, blocking collectives: 17.8 us -> none  [exchange(): return lax.all_to_all(x, 'space', split_axis=0, concat_axis=0, tiled=True)]
    dot_general x19 -> x15, matrix products: 62.7 us -> 48.3 us  [dot(): return lax.dot_general(a, b, (dims, ((), ())), preferred_element_type=F32)]
    convert_element_type x4 -> x0, local copies, waits for them, and re-layouts: 12.4 us -> none  [the longest x3 9.51 us: per_device(): v.astype(BF16).reshape(lines.shape[0], FRAG * SEG, wide)]
  transfers between devices with their start and end apart: 5 -> 1, of which waited for: 4 -> 1; matrix products, arithmetic and copies ran while one was open for 11% -> 5% of each run, Pallas kernels for 0% -> 0%
where the time goes in v2:
time: 373 us
  Pallas kernels  143 us (38%)
  waiting for transfers between devices  76.3 us (20%)
  blocking collectives  70.4 us (19%)
  matrix products  48.3 us (13%)
  between operations  18.2 us (5%)
  other arithmetic  15.3 us (4%)
    pallas_call x1, Pallas kernels, forward_lines(): pl.pallas_call(functools.partial(forward_kernel, cap, scale), out_shape=(...  78 us
    psum x1, waiting for transfers between devices, per_device(): lax.psum((grad_qkv, jnp.stack([grad_gain_attn, grad_gain_mlp])), ('space'...  76.3 us
    psum x1, blocking collectives, per_device(): lax.psum((grad_qkv, jnp.stack([grad_gain_attn, grad_gain_mlp])), ('space'...  70.4 us
    pallas_call x1, Pallas kernels, backward_lines(): pl.pallas_call(functools.partial(backward_kernel, cap, scale), out_shape=...  65 us
    dot_general x15, matrix products, dot(): return lax.dot_general(a, b, (dims, ((), ())), preferred_element_type=F32)  48.3 us
  transfers between devices with their start and end apart: 1, of which 1 were waited for; matrix products, arithmetic and copies ran while one was open for 5% of the time, Pallas kernels for 0%

profile of v2, /device:TPU:1, one launch (start us, length us, event | category | flops | bytes accessed | tf_op | source)
XLA Modules:
  0.0 372.8 jit_solution(8516798253259079045)
XLA Ops:
  7.2 1.0 convert_reduce_fusion.3
  12.3 0.9 convert_reduce_fusion.2
  15.3 2.6 fusion.44
  19.5 2.9 convolution_convert_fusion
  22.5 78.0 %forward_lines.1 = (bf16[16,48,512]{2,1,0:T(8,128)(2,1)}, bf16[8,384,384]{2,1,0:T(8,128)(2,1)}, s32[8,128]{1,0:T(8,128)}) custom-call(bf16[16,48,1536]{2,1,0:T(8,128)(2,1)} %bitcast.39, s32[16,8,128]{2,1,0:T(8,128)} %broadcast_select_fusion.tagt), custom_call_target="tpu_custom_call" | custom-call | tf_op jit(solution)/shard_map/forward_lines/pallas_call | solution.py:283
  100.4 2.0 convert_reduce_fusion
  102.7 1.9 fusion.66
  104.7 3.6 convolution_convert_fusion.1
  108.4 5.2 %fusion.9 = bf16[768,2048]{1,0:T(8,128)(2,1)S(1)} fusion(f32[768,2048]{1,0:T(8,128)S(1)} %fusion.66, bf16[768,512]{0,1:T(8,128)(2,1)S(1)} %copy-done.7, bf16[2048,512]{1,0:T(8,128)(2,1)S(1)} %copy-done.10), kind=kOutput, calls=%fused_computation.11 | convolution fusion | flops 1638924288 | bytes 12320768 | tf_op jit(solution)/shard_map/dot_general | solution.py:25
  113.5 2.1 fusion.28
  115.6 3.2 convolution_convert_fusion.2
  120.0 1.4 convolution_convert_fusion.8
  121.4 1.5 convolution_convert_fusion.5
  122.9 65.0 %backward_lines.1 = bf16[16,48,1536]{2,1,0:T(8,128)(2,1)} custom-call(bf16[16,48,512]{2,1,0:T(8,128)(2,1)} %bitcast.36, bf16[8,384,384]{2,1,0:T(8,128)(2,1)} %get-tuple-element.12.lines, s32[8,128]{1,0:T(8,128)} %get-tuple-element.13.table), custom_call_target="tpu_custom_call" | custom-call | tf_op jit(solution)/shard_map/backward_lines/pallas_call | solution.py:311
  187.9 4.5 %convolution_convert_fusion.3 = bf16[512,1536]{1,0:T(8,128)(2,1)} fusion(bf16[768,1536]{1,0:T(8,128)(2,1)} %bitcast.37, bf16[768,512]{0,1:T(8,128)(2,1)} %copy-done.5, f32[512]{0:T(512)S(1)} %copy-done.13, f32[768]{0:T(1024)S(1)} %add_rsqrt_fusion.1, f32[768]{0:T(1024)S(1)} %broadcast_multiply_fusion.5), kind=kOutput, calls=%fused_computation.19 | convolution fusion | flops 1210712064 | bytes 4726784 | tf_op jit(solution)/shard_map/dot_general | solution.py:25
  192.4 4.8 %fusion.37 = (f32[512]{0:T(512)S(1)}, f32[768]{0:T(1024)S(1)}, f32[768]{0:T(1024)S(1)}, bf16[768,512]{0,1:T(8,128)(2,1)}) fusion(bf16[768,512]{0,1:T(8,128)(2,1)} %copy-done.5, f32[768]{0:T(1024)S(1)} %add_rsqrt_fusion.1, f32[768]{0:T(1024)S(1)} %broadcast_multiply_fusion.5, f32[512]{0:T(512)S(1)} %copy-done.13, bf16[768,1536]{1,0:T(8,128)(2,1)} %bitcast.38, ...), kind=kOutput, calls=%fused_computation.55 | convolution fusion | flops 1212282880 | bytes 5521408 | tf_op jit(solution)/shard_map/dot_general | solution.py:25
  197.3 70.4 %psum.35 = f32[2,512]{1,0:T(2,128)S(1)} all-reduce(f32[2,512]{1,0:T(2,128)S(1)} %pad_maximum_fusion), channel_id=1, replica_groups=mesh['space'=64,'dp'=2] {'space','dp'}, use_global_device_ids=true, to_apply=%region_16.17 | all-reduce | flops 1024 | bytes 8192 | tf_op jit(solution)/shard_map/psum | solution.py:391
  268.3 3.8 %fusion.46 = bf16[1,512,512]{2,1,0:T(8,128)(2,1)} fusion(f32[768,512]{0,1:T(8,128)} %copy-done.1, bf16[768,512]{0,1:T(8,128)(2,1)} %copy-done.5, bf16[768,512]{0,1:T(8,128)(2,1)} %get-tuple-element.39, f32[768]{0:T(1024)S(1)} %broadcast_multiply_fusion, f32[768]{0:T(1024)S(1)} %broadcast_multiply_fusion.1, f32[512]{0:T(512)S(1)} %copy-done.13, ...), kind=kOutput, calls=%fused_computation.71 | convolution fusion | flops 408027136 | bytes 3686400 | tf_op jit(solution)/shard_map/dot_general | solution.py:25
  272.0 8.1 %fusion.45 = bf16[1,512,512]{2,1,0:T(8,128)(2,1)} fusion(s32[512]{0:T(512)S(1)} %add.159, bf16[768,512]{0,1:T(8,128)(2,1)S(1)} %get-tuple-element.37, bf16[2048,512]{1,0:T(8,128)(2,1)} %param.19, f32[768,2048]{1,0:T(8,128)} %copy-done.14), kind=kOutput, calls=%fused_computation.70 | convolution fusion | flops 2029649920 | bytes 9701376 | tf_op jit(solution)/shard_map/dot_general | solution.py:25
  280.1 76.3 %all-reduce.4.cloned.1.call-done = (bf16[512,1536]{1,0:T(8,128)(2,1)}, bf16[512,512]{1,0:T(8,128)(2,1)}, bf16[512,2048]{1,0:T(8,128)(2,1)}, bf16[2048,512]{1,0:T(8,128)(2,1)}) async-done(((bf16[512,1536]{1,0:T(8,128)(2,1)}, bf16[512,512]{1,0:T(8,128)(2,1)}, bf16[512,2048]{1,0:T(8,128)(2,1)}, bf16[2048,512]{1,0:T(8,128)(2,1)}), (bf16[512,1536]{1,0:T(8,128)(2,1)}, bf16[512,512]{1,0:T(8,128)(2,1)}, ...) | async-done | bytes 6291472 | tf_op jit(solution)/shard_map/psum | solution.py:391
  356.4 2.3 convert_multiply_fusion.5
  358.7 2.1 convert_multiply_fusion.2
  360.8 2.6 convert_multiply_fusion.1
  363.4 2.6 convert_multiply_fusion
  (60 shorter events, 5.9 us)
Async XLA Ops:
  7.2 95.6 %copy-start = (bf16[512,2048]{1,0:T(8,128)(2,1)S(1)}, bf16[512,2048]{1,0:T(8,128)(2,1)}, u32[]{:S(2)}) copy-start(bf16[512,2048]{1,0:T(8,128)(2,1)} %param.18) | copy-start | bytes 6291460
  7.2 10.7 %copy-start.12 = (bf16[1,512,512]{2,1,0:T(8,128)(2,1)S(1)}, bf16[1,512,512]{2,1,0:T(8,128)(2,1)}, u32[]{:S(2)}) copy-start(bf16[1,512,512]{2,1,0:T(8,128)(2,1)} %param.10) | copy-start | bytes 1572868
  7.2 349.2 %all-reduce.4.cloned.1.call-start = ((), (), s32[]{:S(2)}) async-start(), calls=%async_computation | async-start | bytes 12582912 | tf_op jit(solution)/shard_map/psum | solution.py:391
  17.9 1.6 copy-start.11
  17.9 1.6 copy-start.13
  18.6 3.9 %copy-start.5 = (bf16[768,512]{0,1:T(8,128)(2,1)}, bf16[768,512]{0,1:T(8,128)(2,1)S(1)}, u32[]{:S(2)}) copy-start(bf16[768,512]{0,1:T(8,128)(2,1)S(1)} %get-tuple-element.35) | copy-start | bytes 2359300
  22.5 78.0 %copy-start.8 = (bf16[512,512]{1,0:T(8,128)(2,1)S(1)}, bf16[512,512]{1,0:T(8,128)(2,1)}, u32[]{:S(2)}) copy-start(bf16[512,512]{1,0:T(8,128)(2,1)} %param.16) | copy-start | bytes 1572868
  100.4 2.3 copy-start.9
  102.7 1.9 copy-start.7
  104.7 3.7 copy-start.14
  104.7 3.7 copy-start.10
  118.8 1.1 copy-start.6
  120.0 2.9 copy-start.1
  356.4 2.3 copy-start.4
  358.7 2.1 copy-start.3
  360.8 2.6 copy-start.2
Sparse Core Ops, SparseCore 0:
  192.5 163.8 all-reduce.3

commit v3 on v2

--- a/solution.py
+++ b/solution.py
@@ -79,7 +79,7 @@
     return ys * 16 + zs * 4 + xs
 
 
-def greet_all(me, count):
+def greet_all(me, count, pair=False):
     barrier = pltpu.get_barrier_semaphore()
 
     def greet(k, carry):
@@ -87,7 +87,9 @@
         return carry
 
     lax.fori_loop(1, count, greet, 0)
-    pl.semaphore_wait(barrier, count - 1)
+    if pair:
+        pl.semaphore_signal(barrier, inc=1, device_id={"dp": 1 - lax.axis_index("dp")}, device_id_type=MESH)
+    pl.semaphore_wait(barrier, count if pair else count - 1)
 
 
 def remote(src, dst, send_sem, recv_sem, device):
@@ -236,14 +238,202 @@
     await_bytes(mixed, sems.at[5])
 
 
-def backward_kernel(cap, scale, dmixed, lines, table, dproj, recv, wide128, gathered, sorter, dlines_in,
-                    dlines, wide32, back, sems):
+VM = pl.BlockSpec(memory_space=pltpu.VMEM)
+
+
+class Reducer:
+    def __init__(self, me, g, out, pair, s0, r1, s1, r2, s2, r3, send, recv):
+        self.me, self.g, self.out, self.pair, self.s0, self.r1, self.s1 = me, g, out, pair, s0, r1, s1
+        self.r2, self.s2, self.r3, self.send, self.recv = r2, s2, r3, send, recv
+        self.core = lax.axis_index("dp")
+        self.place = (lax.div(me, 16), lax.rem(lax.div(me, 4), 4), lax.rem(me, 4))
+
+    def peers(self, axis):
+        step = (16, 4, 1)[axis]
+        mine = self.place[axis]
+        for k in (1, 2, 3):
+            there = lax.rem(mine + k, 4)
+            yield k - 1, there, self.me + (there - mine) * step
+
+    def copy(self, stage, p, src, dst, device):
+        pltpu.make_async_remote_copy(
+            src_ref=src, dst_ref=dst, send_sem=self.send.at[stage, p], recv_sem=self.recv.at[stage, p],
+            device_id=device, device_id_type=MESH,
+        ).start()
+
+    def wait(self, stage, p):
+        await_bytes(self.sized(stage, p), self.recv.at[stage, p])
+
+    def sized(self, stage, p):
+        return (self.pair, self.r1, self.r2, self.r3, self.r3, self.r2, self.r1, self.pair)[stage].at[p]
+
+    def start(self):
+        for p in range(3):
+            self.copy(0, p, self.g.at[1 - self.core, p], self.pair.at[p], {"dp": 1 - self.core})
+
+    def step(self, stage):
+        for p in range(3):
+            self.wait(stage, p)
+            a, b, c = p, (p + 1) % 3, (p + 2) % 3
+            ia, ib, ic = self.place[a], self.place[b], self.place[c]
+            shard = pl.ds(pl.multiple_of(ic * 128, 128), 128)
+            own = self.out.at[self.core, p]
+            if stage == 0:
+
+                def add(i, carry):
+                    u, v = lax.div(i, 4), lax.rem(i, 4)
+                    self.s0[p, u, v] = (self.g[self.core, p, u, v].astype(F32) + self.pair[p, u, v].astype(F32)).astype(BF16)
+                    return carry
+
+                lax.fori_loop(0, 16, add, 0)
+                for k, there, device in self.peers(a):
+                    self.copy(1, p, self.s0.at[p, there], self.r1.at[p, k], {"space": device})
+            elif stage == 1:
+
+                def add4(u, carry):
+                    total = self.s0[p, ia, u].astype(F32)
+                    for k in range(3):
+                        total += self.r1[p, k, u].astype(F32)
+                    self.s1[p, u] = total.astype(BF16)
+                    return carry
+
+                lax.fori_loop(0, 4, add4, 0)
+                for k, there, device in self.peers(b):
+                    self.copy(2, p, self.s1.at[p, there], self.r2.at[p, k], {"space": device})
+            elif stage == 2:
+                total = self.s1[p, ib].astype(F32)
+                for k in range(3):
+                    total += self.r2[p, k].astype(F32)
+                self.s2[p] = total.astype(BF16)
+                for k, there, device in self.peers(c):
+                    part = pl.ds(pl.multiple_of(there * 128, 128), 128)
+                    self.copy(3, p, self.s2.at[p, :, part], self.r3.at[p, k], {"space": device})
+            elif stage == 3:
+                total = self.s2[p, :, shard].astype(F32)
+                for k in range(3):
+                    total += self.r3[p, k].astype(F32)
+                own[ia, ib, :, shard] = total.astype(BF16)
+                for k, there, device in self.peers(c):
+                    piece = own.at[ia, ib, :, shard]
+                    self.copy(4, p, piece, piece, {"space": device})
+            elif stage == 4:
+                for k, there, device in self.peers(b):
+                    self.copy(5, p, own.at[ia, ib], own.at[ia, ib], {"space": device})
+            elif stage == 5:
+                for k, there, device in self.peers(a):
+                    self.copy(6, p, own.at[ia], own.at[ia], {"space": device})
+            elif stage == 6:
+                self.copy(7, p, own, own, {"dp": 1 - self.core})
+
+    def finish(self):
+        for stage in range(8):
+            for p in range(3):
+                await_bytes(self.sized(stage, p), self.send.at[stage, p])
+
+
+def reducer_scratch(q):
+    return [
+        pltpu.VMEM((3, 4, 4, q, 512), BF16),
+        pltpu.VMEM((3, 4, 4, q, 512), BF16),
+        pltpu.VMEM((3, 3, 4, q, 512), BF16),
+        pltpu.VMEM((3, 4, q, 512), BF16),
+        pltpu.VMEM((3, 3, q, 512), BF16),
+        pltpu.VMEM((3, q, 512), BF16),
+        pltpu.VMEM((3, 3, q, 128), BF16),
+        pltpu.SemaphoreType.DMA((8, 3)),
+        pltpu.SemaphoreType.DMA((8, 3)),
+    ]
+
+
+def sum_gains(stage, reducer, got, sems):
+    slots, held, send, recv = got, sems[0], sems[1], sems[2]
+    count = 2 if stage == 0 else 4
+    mine = reducer.core if stage == 0 else reducer.place[stage - 1]
+    slots[stage, mine] = held[stage]
+    if stage == 0:
+        pltpu.make_async_remote_copy(
+            src_ref=held.at[0], dst_ref=slots.at[0, mine], send_sem=send.at[0], recv_sem=recv.at[0],
+            device_id={"dp": 1 - mine}, device_id_type=MESH,
+        ).start()
+    else:
+        for k, there, device in reducer.peers(stage - 1):
+            remote(held.at[stage], slots.at[stage, mine], send.at[stage], recv.at[stage], device).start()
+
+
+def gather_gains(stage, got, sems):
+    slots, held, send, recv = got, sems[0], sems[1], sems[2]
+    count = 2 if stage == 0 else 4
+    await_bytes(slots.at[stage, pl.ds(0, count - 1)], recv.at[stage])
+    total = slots[stage, 0]
+    for k in range(1, count):
+        total += slots[stage, k]
+    return total
+
+
+def tail_kernel(g, gains, out, gains_out, *scratch):
+    me = lax.axis_index("space")
+    red = Reducer(me, g, out, *scratch[:9])
+    slots, held, gsend, grecv = scratch[9:]
+    sems = (held, gsend, grecv)
+    barrier = pltpu.get_barrier_semaphore()
+    pl.semaphore_signal(barrier, inc=1, device_id={"dp": 1 - red.core}, device_id_type=MESH)
+    for axis in range(3):
+        for k, there, device in red.peers(axis):
+            pl.semaphore_signal(barrier, inc=1, device_id={"space": device}, device_id_type=MESH)
+    pl.semaphore_wait(barrier, 10)
+    red.start()
+    held[0] = gains[...]
+    sum_gains(0, red, slots, sems)
+    for stage in range(7):
+        red.step(stage)
+        if stage < 4:
+            total = gather_gains(stage, slots, sems)
+            if stage < 3:
+                held[stage + 1] = total
+                sum_gains(stage + 1, red, slots, sems)
+            else:
+                gains_out[...] = total
+    for p in range(3):
+        red.wait(7, p)
+    red.finish()
+    for stage in range(4):
+        await_bytes(slots.at[stage, pl.ds(0, 1 if stage == 0 else 3)], gsend.at[stage])
+
+
+def reduce_tail(g, gains):
+    q = g.shape[0] // 96
+    out, gains = pl.pallas_call(
+        tail_kernel,
+        out_shape=(
+            jax.ShapeDtypeStruct((2, 3, 4, 4, q, 512), BF16),
+            jax.ShapeDtypeStruct((8, 128), F32),
+        ),
+        in_specs=[VM] * 2,
+        out_specs=(VM,) * 2,
+        scratch_shapes=reducer_scratch(q)
+        + [
+            pltpu.VMEM((4, 4, 8, 128), F32),
+            pltpu.VMEM((4, 8, 128), F32),
+            pltpu.SemaphoreType.DMA((4,)),
+            pltpu.SemaphoreType.DMA((4,)),
+        ],
+        compiler_params=pltpu.CompilerParams(collective_id=3, has_side_effects=True, vmem_limit_bytes=60 << 20),
+        name="reduce_tail",
+    )(g.reshape(2, 3, 4, 4, q, 512), gains)
+    return out.reshape(g.shape), gains
+
+
+def backward_kernel(cap, scale, dmixed, lines, table, g, dproj, out, recv, wide128, gathered, sorter, dlines_in,
+                    dlines, wide32, back, sems, *scratch):
     me = lax.axis_index("space")
     count = recv.shape[0]
-    greet_all(me, count)
+    red = Reducer(me, g, out, *scratch)
+    greet_all(me, count, True)
     send_to_lines(me, count, 1, dmixed, recv, sems.at[0], sems.at[1])
+    red.start()
     build_sorter(table[...], sorter)
     await_bytes(recv, sems.at[1])
+    red.step(0)
     sort_blocks(cap, recv, wide128, gathered, sorter, dlines_in)
     n = TILE * SEG
     mask = same_line()
@@ -266,15 +456,21 @@
             )
         return carry
 
-    lax.fori_loop(0, cap * count // TILE, attend, 0)
+    tiles = cap * count // TILE
+    lax.fori_loop(0, tiles // 2, attend, 0)
+    red.step(1)
+    lax.fori_loop(tiles // 2, tiles, attend, 0)
+    red.step(2)
     unsort_blocks(cap, dlines, wide32, sorter, back)
     send_home(me, count, 3, back, dproj, sems.at[2], sems.at[3])
+    for stage in range(3, 7):
+        red.step(stage)
     await_bytes(recv.at[pl.ds(0, count - 1)], sems.at[0])
     await_bytes(back.at[pl.ds(0, count - 1)], sems.at[2])
     await_bytes(dproj, sems.at[3])
-
-
-VM = pl.BlockSpec(memory_space=pltpu.VMEM)
+    for p in range(3):
+        red.wait(7, p)
+    red.finish()
 
 
 def forward_lines(proj, tagt, cap, count, scale):
@@ -305,14 +501,18 @@
     )(proj, tagt)
 
 
-def backward_lines(dmixed, lines, table, cap, count, scale):
+def backward_lines(dmixed, lines, table, g, cap, count, scale):
+    q = g.shape[0] // 96
     n = cap * count
     span = cap * SEG
-    return pl.pallas_call(
+    dproj, out = pl.pallas_call(
         functools.partial(backward_kernel, cap, scale),
-        out_shape=jax.ShapeDtypeStruct((BINS, span, 1536), BF16),
-        in_specs=[VM] * 3,
-        out_specs=VM,
+        out_shape=(
+            jax.ShapeDtypeStruct((BINS, span, 1536), BF16),
+            jax.ShapeDtypeStruct((2, 3, 4, 4, q, 512), BF16),
+        ),
+        in_specs=[VM] * 4,
+        out_specs=(VM,) * 2,
         scratch_shapes=[
             pltpu.VMEM((count, span, 128), BF16),
             pltpu.VMEM((1, count * span, 128), F32),
@@ -323,10 +523,12 @@
             pltpu.VMEM((3, count * span, 128), F32),
             pltpu.VMEM((count, span, 384), BF16),
             pltpu.SemaphoreType.DMA((4,)),
-        ],
+        ]
+        + reducer_scratch(q),
         compiler_params=pltpu.CompilerParams(collective_id=2, has_side_effects=True, vmem_limit_bytes=60 << 20),
         name="backward_lines",
-    )(dmixed, lines, table)
+    )(dmixed, lines, table, g.reshape(2, 3, 4, 4, q, 512))
+    return dproj, out.reshape(g.shape)
 
 
 def per_device(
@@ -375,30 +577,38 @@
     dhidden = upstream.astype(F32) + norm_back(unit_m, inv_m, gain_mlp, dnormed_mlp)
     dhidden_b = dhidden.astype(BF16)
     dmixed = dot(dhidden_b, w_out, NT).astype(BF16)
-    grad_down = dot(activated, upstream, TN).astype(BF16)
-    grad_up = dot(normed_mlp, dpre, TN).astype(BF16)
-    grad_out = dot(mixed, dhidden_b, TN).astype(BF16)
-    grad_down, grad_up, grad_out = lax.psum((grad_down, grad_up, grad_out), ("space", "dp"))
-
-    dprojected = backward_lines(dmixed.reshape(BINS, span, width), lines, table, cap, nspace, scale)
+    early = [dot(activated, upstream, TN)]
+    early += [dot(normed_mlp, dpre[:, j * width : (j + 1) * width], TN) for j in range(4)]
+    early += [dot(mixed, dhidden_b, TN)]
+    early = jnp.concatenate([v.astype(BF16) for v in early], axis=0)
+
+    dprojected, early = backward_lines(dmixed.reshape(BINS, span, width), lines, table, early, cap, nspace, scale)
     dprojected = dprojected.reshape(BINS * span, 3 * width)
-    grad_qkv = dot(normed, dprojected, TN).astype(BF16)
+    late = [dot(normed, dprojected[:, j * width : (j + 1) * width], TN) for j in range(3)]
+    late = jnp.concatenate([v.astype(BF16) for v in late], axis=0)
     dnormed = dot(dprojected, w_qkv, NT).astype(BF16).astype(F32)
     grad_gain_attn = jnp.sum(unit_a * dnormed, axis=0)
     grad_states = (dhidden + norm_back(unit_a, inv_a, gain_attn, dnormed)).astype(BF16)
     output = dot(pack, output, TN).astype(BF16)
     grad_states = dot(pack, grad_states, TN).astype(BF16)
-    grad_qkv, grad_gains = lax.psum((grad_qkv, jnp.stack([grad_gain_attn, grad_gain_mlp])), ("space", "dp"))
+    late, gains = reduce_tail(late, jnp.concatenate([grad_gain_attn, grad_gain_mlp]).reshape(8, 128))
     factor = 1.0 / math.sqrt(total_rows)
+    gains = gains.reshape(2, width) * factor
+    hidden_units = w_up.shape[1]
+
+    def columns(blocks):
+        blocks = blocks.reshape(-1, width, width)
+        return jnp.concatenate([blocks[j].astype(F32) * factor for j in range(blocks.shape[0])], axis=1)
+
     return (
         output[None],
         grad_states[None],
-        grad_gains[0] * factor,
-        grad_qkv.astype(F32) * factor,
-        grad_out.astype(F32) * factor,
-        grad_gains[1] * factor,
-        grad_up.astype(F32) * factor,
-        grad_down.astype(F32) * factor,
+        gains[0],
+        columns(late),
+        early[2 * hidden_units :].astype(F32) * factor,
+        gains[1],
+        columns(early[hidden_units : 2 * hidden_units]),
+        early[:hidden_units].astype(F32) * factor,
     )
 
 

time: 373 us -> 290 us (0.78)
  waiting for transfers between devices: 76.3 us -> 0 us
  blocking collectives: 70.4 us -> 0 us
  Pallas kernels: 143 us -> 210 us
  between operations: 18.2 us -> 4.85 us
  matrix products: 48.3 us -> 53.2 us
  other arithmetic: 15.3 us -> 19.3 us
    psum x1 -> x0, waiting for transfers between devices: 76.3 us -> none  [per_device(): lax.psum((grad_qkv, jnp.stack([grad_gain_attn, grad_gain_mlp])), ('space'...]
    psum x1 -> x0, blocking collectives: 70.4 us -> none  [per_device(): lax.psum((grad_qkv, jnp.stack([grad_gain_attn, grad_gain_mlp])), ('space'...]
    pallas_call x0 -> x1, Pallas kernels: none -> 34.3 us  [reduce_tail(): pl.pallas_call(tail_kernel, out_shape=(jax.ShapeDtypeStruct((2, 3, 4, 4,...]
    pallas_call x1, Pallas kernels: 65 us -> 96.5 us  [backward_lines(): pl.pallas_call(functools.partial(backward_kernel, cap, scale), out_shape=...]
    concatenate x0 -> x4, other arithmetic: none -> 6.11 us  [the longest x2 4.26 us: columns(): jnp.concatenate([blocks[j].astype(F32) * factor for j in range(blocks.sha...]
    dot_general x15 -> x20, matrix products: 48.3 us -> 53.2 us  [dot(): return lax.dot_general(a, b, (dims, ((), ())), preferred_element_type=F32)]
    mul x5 -> x4, other arithmetic: 10.1 us -> 6.85 us  [the longest x2 3.55 us: columns(): blocks[j].astype(F32) * factor]
  transfers between devices with their start and end apart: 1 -> 0, of which waited for: 1 -> 0; matrix products, arithmetic and copies ran while one was open for 5% -> 0% of each run, Pallas kernels for 0% -> 0%
where the time goes in v3:
time: 290 us
  Pallas kernels  210 us (72%)
  matrix products  53.2 us (18%)
  other arithmetic  19.3 us (7%)
  between operations  4.85 us (2%)
    pallas_call x1, Pallas kernels, backward_lines(): pl.pallas_call(functools.partial(backward_kernel, cap, scale), out_shape=...  96.5 us
    pallas_call x1, Pallas kernels, forward_lines(): pl.pallas_call(functools.partial(forward_kernel, cap, scale), out_shape=(...  78.7 us
    dot_general x20, matrix products, dot(): return lax.dot_general(a, b, (dims, ((), ())), preferred_element_type=F32)  53.2 us
    pallas_call x1, Pallas kernels, reduce_tail(): pl.pallas_call(tail_kernel, out_shape=(jax.ShapeDtypeStruct((2, 3, 4, 4,...  34.3 us

profile of v3, /device:TPU:1, one launch (start us, length us, event | category | flops | bytes accessed | tf_op | source)
XLA Modules:
  0.0 289.7 jit_solution(18059967869710840585)
XLA Ops:
  9.4 2.6 fusion.45
  13.4 2.9 %convolution_convert_fusion = bf16[768,1536]{1,0:T(8,128)(2,1)} fusion(bf16[512,1536]{1,0:T(8,128)(2,1)S(1)} %copy-done.10, bf16[768,512]{0,1:T(8,128)(2,1)S(1)} %get-tuple-element.47, f32[512]{0:T(512)S(1)} %copy-done.13, f32[768]{0:T(1024)S(1)} %add_rsqrt_fusion.1, f32[768]{0:T(1024)S(1)} %broadcast_multiply_fusion.6), kind=kOutput, calls=%fused_computation.15 | convolution fusion | flops 1211105280 | bytes 4726784 | tf_op jit(solution)/shard_map/dot_general | solution.py:25
  16.3 78.7 %forward_lines.1 = (bf16[16,48,512]{2,1,0:T(8,128)(2,1)}, bf16[8,384,384]{2,1,0:T(8,128)(2,1)}, s32[8,128]{1,0:T(8,128)}) custom-call(bf16[16,48,1536]{2,1,0:T(8,128)(2,1)} %bitcast.52, s32[16,8,128]{2,1,0:T(8,128)} %broadcast_select_fusion.tagt), custom_call_target="tpu_custom_call" | custom-call | tf_op jit(solution)/shard_map/forward_lines/pallas_call | solution.py:479
  95.1 2.0 convert_reduce_fusion
  97.4 4.6 %fusion.91 = f32[768,2048]{1,0:T(8,128)} fusion(bf16[512,2048]{1,0:T(8,128)(2,1)S(1)} %copy-done, bf16[768,512]{0,1:T(8,128)(2,1)S(1)} %get-tuple-element.49, f32[512]{0:T(512)S(1)} %copy-done.8, f32[768]{0:T(1024)S(1)} %add_rsqrt_fusion, f32[768]{0:T(1024)S(1)} %broadcast_multiply_fusion.5), kind=kOutput, calls=%fused_computation.149 | convolution fusion | flops 1612578816 | bytes 9183232 | tf_op jit(solution)/shard_map/dot_general | solution.py:25
  102.0 8.0 %fusion.51 = bf16[1,512,512]{2,1,0:T(8,128)(2,1)} fusion(s32[512]{0:T(512)S(1)} %add.149, bf16[768,512]{0,1:T(8,128)(2,1)S(1)} %get-tuple-element.49, bf16[2048,512]{1,0:T(8,128)(2,1)} %param.19, f32[768,2048]{1,0:T(8,128)} %fusion.91), kind=kOutput, calls=%fused_computation.82 | convolution fusion | flops 2029649920 | bytes 9701376 | tf_op jit(solution)/shard_map/dot_general | solution.py:25
  110.0 8.5 %fusion.9 = bf16[768,2048]{1,0:T(8,128)(2,1)S(1)} fusion(f32[768,2048]{1,0:T(8,128)} %fusion.91, bf16[768,512]{0,1:T(8,128)(2,1)} %fusion.45, bf16[2048,512]{1,0:T(8,128)(2,1)} %param.19), kind=kOutput, calls=%fused_computation.11 | convolution fusion | flops 1638924288 | bytes 12320768 | tf_op jit(solution)/shard_map/dot_general | solution.py:25
  118.6 3.7 %fusion.10 = bf16[4608,512]{1,0:T(8,128)(2,1)} fusion(bf16[768,512]{0,1:T(8,128)(2,1)S(1)} %copy-done.5, f32[768,2048]{1,0:T(8,128)S(1)} %copy-done.14), kind=kOutput, calls=%fused_computation.18 | convolution fusion | flops 1625817088 | bytes 9175040 | tf_op jit(solution)/shard_map/dot_general | solution.py:25
  122.2 1.4 fusion.50
  126.5 1.5 fusion.47
  128.0 2.1 fusion.29
  130.1 1.8 fusion.28
  131.9 1.5 fusion.46
  133.4 1.5 convolution_convert_fusion.3
  134.9 96.5 %backward_lines.1 = (bf16[16,48,1536]{2,1,0:T(8,128)(2,1)}, bf16[2,3,4,4,48,512]{5,4,3,2,1,0:T(8,128)(2,1)}) custom-call(bf16[16,48,512]{2,1,0:T(8,128)(2,1)} %bitcast.51, bf16[8,384,384]{2,1,0:T(8,128)(2,1)} %get-tuple-element.16.lines, s32[8,128]{1,0:T(8,128)} %get-tuple-element.17.table, bf16[2,3,4,4,48,512]{5,4,3,2,1,0:T(8,128)(2,1)} %bitcast.6.g), custom_call_target="tpu_custom_call" | custom-call | tf_op jit(solution)/shard_map/backward_lines/pallas_call | solution.py:508
  231.4 2.1 convolution_convert_fusion.6
  235.8 2.5 fusion.38
  240.2 34.3 %reduce_tail.1 = (bf16[2,3,4,4,16,512]{5,4,3,2,1,0:T(8,128)(2,1)}, f32[8,128]{1,0:T(8,128)}) custom-call(bf16[2,3,4,4,16,512]{5,4,3,2,1,0:T(8,128)(2,1)} %bitcast.46, f32[8,128]{1,0:T(8,128)} %pad_maximum_fusion.3.gains), custom_call_target="tpu_custom_call" | custom-call | tf_op jit(solution)/shard_map/reduce_tail/pallas_call | solution.py:405
  275.8 3.4 %fusion.52 = bf16[1,512,512]{2,1,0:T(8,128)(2,1)} fusion(f32[768,512]{0,1:T(8,128)S(1)} %fusion.28, bf16[768,512]{0,1:T(8,128)(2,1)} %copy-done.2, bf16[768,512]{0,1:T(8,128)(2,1)} %get-tuple-element.51, f32[768]{0:T(1024)S(1)} %broadcast_multiply_fusion.1, f32[768]{0:T(1024)S(1)} %broadcast_multiply_fusion.2, f32[512]{0:T(512)S(1)} %copy-done.13, ...), kind=kOutput, calls=%fused_computation.83 | convolution fusion | flops 408027136 | bytes 3686400 | tf_op jit(solution)/shard_map/dot_general | solution.py:25
  279.2 1.8 multiply_bitcast_fusion.2
  281.1 1.9 pad_maximum_fusion.1
  283.0 2.6 convert_multiply_fusion
  285.6 1.7 convert_multiply_fusion.6
  287.3 2.4 pad_maximum_fusion
  (70 shorter events, 14.7 us)
Async XLA Ops:
  0.6 96.7 %copy-start = (bf16[512,2048]{1,0:T(8,128)(2,1)S(1)}, bf16[512,2048]{1,0:T(8,128)(2,1)}, u32[]{:S(2)}) copy-start(bf16[512,2048]{1,0:T(8,128)(2,1)} %param.18) | copy-start | bytes 6291460
  0.6 11.3 %copy-start.12 = (bf16[1,512,512]{2,1,0:T(8,128)(2,1)S(1)}, bf16[1,512,512]{2,1,0:T(8,128)(2,1)}, u32[]{:S(2)}) copy-start(bf16[1,512,512]{2,1,0:T(8,128)(2,1)} %param.10) | copy-start | bytes 1572868
  12.0 1.4 copy-start.10
  12.0 1.4 copy-start.13
  12.6 3.7 %copy-start.2 = (bf16[768,512]{0,1:T(8,128)(2,1)}, bf16[768,512]{0,1:T(8,128)(2,1)S(1)}, u32[]{:S(2)}) copy-start(bf16[768,512]{0,1:T(8,128)(2,1)S(1)} %get-tuple-element.47) | copy-start | bytes 2359300
  16.3 78.7 %copy-start.6 = (bf16[512,512]{1,0:T(8,128)(2,1)S(1)}, bf16[512,512]{1,0:T(8,128)(2,1)}, u32[]{:S(2)}) copy-start(bf16[512,512]{1,0:T(8,128)(2,1)} %param.16) | copy-start | bytes 1572868
  95.1 2.3 copy-start.8
  97.1 30.9 %copy-start.1 = (bf16[768,512]{0,1:T(8,128)(2,1)}, bf16[768,512]{0,1:T(8,128)(2,1)S(1)}, u32[]{:S(2)}) copy-start(bf16[768,512]{0,1:T(8,128)(2,1)S(1)} %get-tuple-element.49) | copy-start | bytes 2359300
  110.0 8.5 %copy-start.5 = (bf16[768,512]{0,1:T(8,128)(2,1)S(1)}, bf16[768,512]{0,1:T(8,128)(2,1)}, u32[]{:S(2)}) copy-start(bf16[768,512]{0,1:T(8,128)(2,1)} %fusion.45) | copy-start | bytes 2359300
  110.0 8.6 %copy-start.14 = (f32[768,2048]{1,0:T(8,128)S(1)}, f32[768,2048]{1,0:T(8,128)}, u32[]{:S(2)}) copy-start(f32[768,2048]{1,0:T(8,128)} %fusion.91) | copy-start | bytes 18874372
  130.1 1.8 copy-start.4
  131.9 1.5 copy-start.7
  231.4 2.2 copy-start.3
  231.4 2.4 copy-start.9
  234.4 1.4 copy-start.11
  275.8 7.2 %slice-start = ((s8[4718592]{0:T(1024)(128)(4,1)}), s8[4194304]{0:T(1024)(128)(4,1)S(1)}, s32[]{:S(2)}) async-start(s8[4718592]{0:T(1024)(128)(4,1)} %bitcast.47), calls=%async_computation | async-start | bytes 8388608
  279.2 3.7 %slice-start.1 = ((s8[4718592]{0:T(1024)(128)(4,1)}), s8[524288]{0:T(1024)(128)(4,1)S(1)}, s32[]{:S(2)}) async-start(s8[4718592]{0:T(1024)(128)(4,1)} %bitcast.47), calls=%async_computation.1 | async-start | bytes 1048576

commit v4 on v3

--- a/solution.py
+++ b/solution.py
@@ -13,7 +13,6 @@
 FRAG = 4
 BINS = 16
 PAIRS = 4
-CAP = 6
 
 EPSILON = 1e-05
 F32 = jnp.float32
@@ -64,6 +63,11 @@
     index = jnp.sum(ahead, axis=1, dtype=jnp.int32)
     n3 = jnp.sum(first & (load == 3), dtype=jnp.int32)
     n2 = jnp.sum(first & (load == 2), dtype=jnp.int32)
+    if cap == 4:
+        spare = index < n3
+        base1 = jnp.where(spare, 4 * index + 3, 3 * n3 + 2 * n2 + index)
+        base = jnp.where(load == 3, 4 * index, jnp.where(load == 2, 4 * n3 + 2 * index, base1))
+        return base + rank, (base % cap) * n + place
     odd = (n3 % 2) == 1
     base3 = 3 * index
     base2 = 3 * n3 + 2 * index + jnp.where(odd & (index >= 1), 1, 0)
@@ -400,7 +404,7 @@
         await_bytes(slots.at[stage, pl.ds(0, 1 if stage == 0 else 3)], gsend.at[stage])
 
 
-def reduce_tail(g, gains):
+def reduce_tail(cap, g, gains):
     q = g.shape[0] // 96
     out, gains = pl.pallas_call(
         tail_kernel,
@@ -417,7 +421,7 @@
             pltpu.SemaphoreType.DMA((4,)),
             pltpu.SemaphoreType.DMA((4,)),
         ],
-        compiler_params=pltpu.CompilerParams(collective_id=3, has_side_effects=True, vmem_limit_bytes=60 << 20),
+        compiler_params=pltpu.CompilerParams(collective_id=20 + cap, has_side_effects=True, vmem_limit_bytes=60 << 20),
         name="reduce_tail",
     )(g.reshape(2, 3, 4, 4, q, 512), gains)
     return out.reshape(g.shape), gains
@@ -496,7 +500,7 @@
             pltpu.VMEM((count, span, 128), BF16),
             pltpu.SemaphoreType.DMA((6,)),
         ],
-        compiler_params=pltpu.CompilerParams(collective_id=1, has_side_effects=True, vmem_limit_bytes=60 << 20),
+        compiler_params=pltpu.CompilerParams(collective_id=cap, has_side_effects=True, vmem_limit_bytes=60 << 20),
         name="forward_lines",
     )(proj, tagt)
 
@@ -525,21 +529,32 @@
             pltpu.SemaphoreType.DMA((4,)),
         ]
         + reducer_scratch(q),
-        compiler_params=pltpu.CompilerParams(collective_id=2, has_side_effects=True, vmem_limit_bytes=60 << 20),
+        compiler_params=pltpu.CompilerParams(collective_id=10 + cap, has_side_effects=True, vmem_limit_bytes=60 << 20),
         name="backward_lines",
     )(dmixed, lines, table, g.reshape(2, 3, 4, 4, q, 512))
     return dproj, out.reshape(g.shape)
 
 
-def per_device(
-    states, cotangent, send_owner, line_place, gain_attn, w_qkv, w_out, gain_mlp, w_up, w_down
+def fits_four(owner):
+    same = owner[:, None] == owner[None, :]
+    load = jnp.sum(same, axis=1, dtype=jnp.int32)
+    threes = jnp.sum(load == 3, dtype=jnp.int32)
+    twos = jnp.sum(load == 2, dtype=jnp.int32)
+    return 4 * threes + 3 * twos <= 3 * owner.shape[0]
+
+
+def per_device(*args):
+    return lax.cond(fits_four(args[2]), functools.partial(block, 4), functools.partial(block, 6), *args)
+
+
+def block(
+    cap, states, cotangent, send_owner, line_place, gain_attn, w_qkv, w_out, gain_mlp, w_up, w_down
 ):
     width = states.shape[2]
     rows = states.shape[1]
     nspace = lax.axis_size("space")
     total_rows = rows * nspace * lax.axis_size("dp")
     nblocks = send_owner.shape[0]
-    cap = CAP
     slots = BINS * cap
     wide = 2 * (width // HEADS)
     head_dim = width // HEADS
@@ -591,7 +606,7 @@
     grad_states = (dhidden + norm_back(unit_a, inv_a, gain_attn, dnormed)).astype(BF16)
     output = dot(pack, output, TN).astype(BF16)
     grad_states = dot(pack, grad_states, TN).astype(BF16)
-    late, gains = reduce_tail(late, jnp.concatenate([grad_gain_attn, grad_gain_mlp]).reshape(8, 128))
+    late, gains = reduce_tail(cap, late, jnp.concatenate([grad_gain_attn, grad_gain_mlp]).reshape(8, 128))
     factor = 1.0 / math.sqrt(total_rows)
     gains = gains.reshape(2, width) * factor
     hidden_units = w_up.shape[1]

time: 290 us -> 250 us (0.86); the launches traced: 290 us -> 246 us
  Pallas kernels: 210 us -> 172 us
  matrix products: 53.2 us -> 41.6 us
  loops' own time: 0 us -> 7.93 us
    pallas_call x1, Pallas kernels: 78.7 us -> 58.7 us  [forward_lines(): pl.pallas_call(functools.partial(forward_kernel, cap, scale), out_shape=(...]
    pallas_call x1, Pallas kernels: 96.5 us -> 80.1 us  [backward_lines(): pl.pallas_call(functools.partial(backward_kernel, cap, scale), out_shape=...]
    dot_general x20, matrix products: 53.2 us -> 41.6 us  [dot(): return lax.dot_general(a, b, (dims, ((), ())), preferred_element_type=F32)]
    another operation x0 -> x1, loops' own time: none -> 7.93 us  [per_device(): lax.cond(fits_four(args[2]), functools.partial(block, 4), functools.parti...]
where the time goes in v4:
time: 250 us; the launch traced here: 246 us
  Pallas kernels  172 us (69%)
  matrix products  41.6 us (17%)
  other arithmetic  18.8 us (8%)
  loops' own time  7.93 us (3%)
  between operations  3.05 us (1%)
    pallas_call x1, Pallas kernels, backward_lines(): pl.pallas_call(functools.partial(backward_kernel, cap, scale), out_shape=...  80.1 us
    pallas_call x1, Pallas kernels, forward_lines(): pl.pallas_call(functools.partial(forward_kernel, cap, scale), out_shape=(...  58.7 us
    dot_general x20, matrix products, dot(): return lax.dot_general(a, b, (dims, ((), ())), preferred_element_type=F32)  41.6 us
    pallas_call x1, Pallas kernels, reduce_tail(): pl.pallas_call(tail_kernel, out_shape=(jax.ShapeDtypeStruct((2, 3, 4, 4,...  33.2 us
    another operation x1, loops' own time, per_device(): lax.cond(fits_four(args[2]), functools.partial(block, 4), functools.parti...  7.93 us

profile of v4, /device:TPU:1, one launch (start us, length us, event | category | flops | bytes accessed | tf_op | source)
XLA Modules:
  0.0 245.6 jit_solution(1552034657191218674)
XLA Ops:
  3.5 241.0 %conditional.1 = (bf16[1,512,512]{2,1,0:T(8,128)(2,1)}, bf16[1,512,512]{2,1,0:T(8,128)(2,1)}, f32[512]{0:T(512)}, f32[512,1536]{1,0:T(8,128)}, f32[512,512]{1,0:...) conditional(s32[]{:T(128)} %convert_element_type.275, (s32[64]{0:T(128)}, ...), branch_computations={%region_3.20_spmd, %region_20.37_spmd} | conditional | flops 16228642816 | bytes 223168768 | solution.py:547
  13.6 1.3 fusion.171
  16.3 2.3 convolution_convert_fusion.28
  18.6 1.6 convert_reduce_fusion.5
  20.4 2.3 convolution_convert_fusion.14
  22.7 58.7 %forward_lines.3 = (bf16[16,32,512]{2,1,0:T(8,128)(2,1)}, bf16[8,256,384]{2,1,0:T(8,128)(2,1)}, s32[8,128]{1,0:T(8,128)}) custom-call(bf16[16,32,1536]{2,1,0:T(8,128)(2,1)} %bitcast.105, s32[16,8,128]{2,1,0:T(8,128)} %broadcast_select_fusion.1.tagt), custom_call_target="tpu_custom_call" | custom-call | tf_op jit(solution)/shard_map/cond/branch_1_fun/forward_lines/pallas_call | solution.py:483
  81.4 1.5 convert_reduce_fusion.4
  83.2 3.4 %fusion.180 = f32[512,2048]{1,0:T(8,128)} fusion(bf16[512,2048]{1,0:T(8,128)(2,1)S(1)} %copy-done.3, bf16[512,512]{0,1:T(8,128)(2,1)S(1)} %get-tuple-element.151, f32[512]{0:T(512)S(1)} %copy-done.16, f32[512]{0:T(512)S(1)} %add_rsqrt_fusion.2, f32[512]{0:T(512)S(1)} %broadcast_multiply_fusion.13), kind=kOutput, calls=%fused_computation.299 | convolution fusion | flops 1075052544 | bytes 6821888 | tf_op jit(solution)/shard_map/cond/branch_1_fun/dot_general | solution.py:24
  86.6 6.1 %fusion.124 = bf16[1,512,512]{2,1,0:T(8,128)(2,1)} fusion(bf16[2048,512]{1,0:T(8,128)(2,1)} %get-tuple-element.66, bf16[512,512]{0,1:T(8,128)(2,1)S(1)} %get-tuple-element.151, s32[512]{0:T(512)S(1)} %add.251, f32[512,2048]{1,0:T(8,128)} %fusion.180), kind=kOutput, calls=%fused_computation.212 | convolution fusion | flops 1353187328 | bytes 7342080 | tf_op jit(solution)/shard_map/cond/branch_1_fun/dot_general | solution.py:24
  92.7 6.2 %fusion.102 = bf16[512,2048]{1,0:T(8,128)(2,1)S(1)} fusion(f32[512,2048]{1,0:T(8,128)} %fusion.180, bf16[512,512]{0,1:T(8,128)(2,1)} %convolution_convert_fusion.28, bf16[2048,512]{1,0:T(8,128)(2,1)} %get-tuple-element.66), kind=kOutput, calls=%fused_computation.161 | convolution fusion | flops 1092616192 | bytes 8912896 | tf_op jit(solution)/shard_map/cond/branch_1_fun/dot_general | solution.py:24
  99.0 3.2 %fusion.103 = bf16[4608,512]{1,0:T(8,128)(2,1)} fusion(bf16[512,512]{0,1:T(8,128)(2,1)S(1)} %copy-done.13, f32[512,2048]{1,0:T(8,128)S(1)} %copy-done), kind=kOutput, calls=%fused_computation.168 | convolution fusion | flops 1084227584 | bytes 6815744 | tf_op jit(solution)/shard_map/cond/branch_1_fun/dot_general | solution.py:24
  102.2 1.3 fusion.107
  104.8 1.3 fusion.109
  106.1 1.3 fusion.110
  107.5 1.5 fusion.131
  110.0 1.4 fusion.111
  112.7 80.1 %backward_lines.3 = (bf16[16,32,1536]{2,1,0:T(8,128)(2,1)}, bf16[2,3,4,4,48,512]{5,4,3,2,1,0:T(8,128)(2,1)}) custom-call(bf16[16,32,512]{2,1,0:T(8,128)(2,1)} %bitcast.104, bf16[8,256,384]{2,1,0:T(8,128)(2,1)} %get-tuple-element.68.lines, s32[8,128]{1,0:T(8,128)} %get-tuple-element.69.table, bf16[2,3,4,4,48,512]{5,4,3,2,1,0:T(8,128)(2,1)} %bitcast.25.g), custom_call_target="tpu_custom_call" | custom-call | tf_op jit(solution)/shard_map/cond/branch_1_fun/backward_lines/pallas_call | solution.py:512
  192.8 1.6 convolution_convert_fusion.18
  199.0 33.2 %reduce_tail.3 = (bf16[2,3,4,4,16,512]{5,4,3,2,1,0:T(8,128)(2,1)}, f32[8,128]{1,0:T(8,128)}) custom-call(bf16[2,3,4,4,16,512]{5,4,3,2,1,0:T(8,128)(2,1)} %bitcast.93, f32[8,128]{1,0:T(8,128)} %pad_maximum_fusion.7.gains), custom_call_target="tpu_custom_call" | custom-call | tf_op jit(solution)/shard_map/cond/branch_1_fun/reduce_tail/pallas_call | solution.py:409
  233.6 1.6 fusion.125
  235.7 1.9 pad_maximum_fusion.5
  237.6 2.6 %convert_multiply_fusion.8 = f32[2048,512]{1,0:T(8,128)} fusion(bf16[4608,512]{1,0:T(8,128)(2,1)S(1)} %bitcast.100), kind=kLoop, calls=%fused_computation.163 | loop fusion | flops 2097152 | bytes 6291456 | tf_op jit(solution)/shard_map/cond/branch_1_fun/mul | solution.py:626
  240.2 1.7 convert_multiply_fusion.14
  241.9 2.4 pad_maximum_fusion.4
  (71 shorter events, 15.9 us)
Async XLA Ops:
  8.9 11.5 %copy-start.20 = (bf16[512,1536]{1,0:T(8,128)(2,1)S(1)}, bf16[512,1536]{1,0:T(8,128)(2,1)}, u32[]{:S(2)}) copy-start(bf16[512,1536]{1,0:T(8,128)(2,1)} %get-tuple-element.60) | copy-start | bytes 4718596 | tf_op jit(solution)/shard_map/cond
  9.0 11.5 %copy-start.25 = (f32[512]{0:T(512)S(1)}, f32[512]{0:T(512)}, u32[]{:S(2)}) copy-start(f32[512]{0:T(512)} %get-tuple-element.59) | copy-start | bytes 6148 | tf_op jit(solution)/shard_map/cond
  20.2 61.2 %copy-start.11 = (bf16[512,512]{0,1:T(8,128)(2,1)}, bf16[512,512]{0,1:T(8,128)(2,1)S(1)}, u32[]{:S(2)}) copy-start(bf16[512,512]{0,1:T(8,128)(2,1)S(1)} %get-tuple-element.149) | copy-start | bytes 1572868 | tf_op jit(solution)/shard_map/cond
  20.4 61.0 %copy-start.5 = (bf16[512,512]{1,0:T(8,128)(2,1)S(1)}, bf16[512,512]{1,0:T(8,128)(2,1)}, u32[]{:S(2)}) copy-start(bf16[512,512]{1,0:T(8,128)(2,1)} %get-tuple-element.63) | copy-start | bytes 1572868 | tf_op jit(solution)/shard_map/cond
  22.7 60.5 %copy-start.3 = (bf16[512,2048]{1,0:T(8,128)(2,1)S(1)}, bf16[512,2048]{1,0:T(8,128)(2,1)}, u32[]{:S(2)}) copy-start(bf16[512,2048]{1,0:T(8,128)(2,1)} %get-tuple-element.65) | copy-start | bytes 6291460 | tf_op jit(solution)/shard_map/cond
  22.7 60.5 %copy-start.16 = (f32[512]{0:T(512)S(1)}, f32[512]{0:T(512)}, u32[]{:S(2)}) copy-start(f32[512]{0:T(512)} %get-tuple-element.64) | copy-start | bytes 6148 | tf_op jit(solution)/shard_map/cond
  92.7 6.2 %copy-start = (f32[512,2048]{1,0:T(8,128)S(1)}, f32[512,2048]{1,0:T(8,128)}, u32[]{:S(2)}) copy-start(f32[512,2048]{1,0:T(8,128)} %fusion.180) | copy-start | bytes 12582916 | tf_op jit(solution)/shard_map/cond
  92.7 6.3 %copy-start.13 = (bf16[512,512]{0,1:T(8,128)(2,1)S(1)}, bf16[512,512]{0,1:T(8,128)(2,1)}, u32[]{:S(2)}) copy-start(bf16[512,512]{0,1:T(8,128)(2,1)} %convolution_convert_fusion.28) | copy-start | bytes 1572868 | tf_op jit(solution)/shard_map/cond
  109.0 1.0 copy-start.14
  109.0 2.4 copy-start.6
  112.7 80.1 %copy-start.12 = (bf16[512,512]{0,1:T(8,128)(2,1)S(1)}, bf16[512,512]{0,1:T(8,128)(2,1)}, u32[]{:S(2)}) copy-start(bf16[512,512]{0,1:T(8,128)(2,1)} %copy-done.11) | copy-start | bytes 1572868 | tf_op jit(solution)/shard_map/cond
  192.8 1.7 copy-start.22
  194.5 1.4 copy-start.21
  232.2 3.0 %copy-start.7 = (bf16[2,3,4,4,16,512]{5,4,3,2,1,0:T(8,128)(2,1)S(1)}, bf16[2,3,4,4,16,512]{5,4,3,2,1,0:T(8,128)(2,1)}, u32[]{:S(2)}) copy-start(bf16[2,3,4,4,16,512]{5,4,3,2,1,0:T(8,128)(2,1)} %get-tuple-element.72) | copy-start | bytes 4718596 | tf_op jit(solution)/shard_map/cond
  233.6 3.9 %slice-start.2 = ((s8[4718592]{0:T(1024)(128)(4,1)}), s8[4194304]{0:T(1024)(128)(4,1)S(1)}, s32[]{:S(2)}) async-start(s8[4718592]{0:T(1024)(128)(4,1)} %bitcast.98), calls=%async_computation.2 | async-start | bytes 8388608 | tf_op jit(solution)/shard_map/cond
  235.2 2.3 slice-start.3

commit v5 on v4

--- a/solution.py
+++ b/solution.py
@@ -249,6 +249,7 @@
     def __init__(self, me, g, out, pair, s0, r1, s1, r2, s2, r3, send, recv):
         self.me, self.g, self.out, self.pair, self.s0, self.r1, self.s1 = me, g, out, pair, s0, r1, s1
         self.r2, self.s2, self.r3, self.send, self.recv = r2, s2, r3, send, recv
+        self.q = s2.shape[1]
         self.core = lax.axis_index("dp")
         self.place = (lax.div(me, 16), lax.rem(lax.div(me, 4), 4), lax.rem(me, 4))
 
@@ -259,6 +260,15 @@
             there = lax.rem(mine + k, 4)
             yield k - 1, there, self.me + (there - mine) * step
 
+    def rows(self, half, p, u=None, v=None):
+        q = self.q
+        start, size = (half * 3 + p) * 16 * q, 16 * q
+        if u is not None:
+            start, size = start + u * 4 * q, 4 * q
+        if v is not None:
+            start, size = start + v * q, q
+        return pl.ds(pl.multiple_of(start, 16), size)
+
     def copy(self, stage, p, src, dst, device):
         pltpu.make_async_remote_copy(
             src_ref=src, dst_ref=dst, send_sem=self.send.at[stage, p], recv_sem=self.recv.at[stage, p],
@@ -273,7 +283,7 @@
 
     def start(self):
         for p in range(3):
-            self.copy(0, p, self.g.at[1 - self.core, p], self.pair.at[p], {"dp": 1 - self.core})
+            self.copy(0, p, self.g.at[self.rows(1 - self.core, p)], self.pair.at[p], {"dp": 1 - self.core})
 
     def step(self, stage):
         for p in range(3):
@@ -281,12 +291,13 @@
             a, b, c = p, (p + 1) % 3, (p + 2) % 3
             ia, ib, ic = self.place[a], self.place[b], self.place[c]
             shard = pl.ds(pl.multiple_of(ic * 128, 128), 128)
-            own = self.out.at[self.core, p]
             if stage == 0:
 
                 def add(i, carry):
                     u, v = lax.div(i, 4), lax.rem(i, 4)
-                    self.s0[p, u, v] = (self.g[self.core, p, u, v].astype(F32) + self.pair[p, u, v].astype(F32)).astype(BF16)
+                    both = self.g[self.rows(self.core, p, u, v)].astype(F32)
+                    both += self.pair[p, pl.ds(pl.multiple_of(i * self.q, 16), self.q)].astype(F32)
+                    self.s0[p, u, v] = both.astype(BF16)
                     return carry
 
                 lax.fori_loop(0, 16, add, 0)
@@ -316,18 +327,21 @@
                 total = self.s2[p, :, shard].astype(F32)
                 for k in range(3):
                     total += self.r3[p, k].astype(F32)
-                own[ia, ib, :, shard] = total.astype(BF16)
+                self.out[self.rows(self.core, p, ia, ib), shard] = total.astype(BF16)
                 for k, there, device in self.peers(c):
-                    piece = own.at[ia, ib, :, shard]
+                    piece = self.out.at[self.rows(self.core, p, ia, ib), shard]
                     self.copy(4, p, piece, piece, {"space": device})
             elif stage == 4:
                 for k, there, device in self.peers(b):
-                    self.copy(5, p, own.at[ia, ib], own.at[ia, ib], {"space": device})
+                    piece = self.out.at[self.rows(self.core, p, ia, ib)]
+                    self.copy(5, p, piece, piece, {"space": device})
             elif stage == 5:
                 for k, there, device in self.peers(a):
-                    self.copy(6, p, own.at[ia], own.at[ia], {"space": device})
+                    piece = self.out.at[self.rows(self.core, p, ia)]
+                    self.copy(6, p, piece, piece, {"space": device})
             elif stage == 6:
-                self.copy(7, p, own, own, {"dp": 1 - self.core})
+                piece = self.out.at[self.rows(self.core, p)]
+                self.copy(7, p, piece, piece, {"dp": 1 - self.core})
 
     def finish(self):
         for stage in range(8):
@@ -337,7 +351,7 @@
 
 def reducer_scratch(q):
     return [
-        pltpu.VMEM((3, 4, 4, q, 512), BF16),
+        pltpu.VMEM((3, 16 * q, 512), BF16),
         pltpu.VMEM((3, 4, 4, q, 512), BF16),
         pltpu.VMEM((3, 3, 4, q, 512), BF16),
         pltpu.VMEM((3, 4, q, 512), BF16),
@@ -409,7 +423,7 @@
     out, gains = pl.pallas_call(
         tail_kernel,
         out_shape=(
-            jax.ShapeDtypeStruct((2, 3, 4, 4, q, 512), BF16),
+            jax.ShapeDtypeStruct(g.shape, BF16),
             jax.ShapeDtypeStruct((8, 128), F32),
         ),
         in_specs=[VM] * 2,
@@ -423,22 +437,11 @@
         ],
         compiler_params=pltpu.CompilerParams(collective_id=20 + cap, has_side_effects=True, vmem_limit_bytes=60 << 20),
         name="reduce_tail",
-    )(g.reshape(2, 3, 4, 4, q, 512), gains)
-    return out.reshape(g.shape), gains
-
-
-def backward_kernel(cap, scale, dmixed, lines, table, g, dproj, out, recv, wide128, gathered, sorter, dlines_in,
-                    dlines, wide32, back, sems, *scratch):
-    me = lax.axis_index("space")
-    count = recv.shape[0]
-    red = Reducer(me, g, out, *scratch)
-    greet_all(me, count, True)
-    send_to_lines(me, count, 1, dmixed, recv, sems.at[0], sems.at[1])
-    red.start()
-    build_sorter(table[...], sorter)
-    await_bytes(recv, sems.at[1])
-    red.step(0)
-    sort_blocks(cap, recv, wide128, gathered, sorter, dlines_in)
+    )(g, gains)
+    return out, gains
+
+
+def backward_tiles(scale, lines, dlines_in, dlines):
     n = TILE * SEG
     mask = same_line()
     low = lax.broadcasted_iota(jnp.int32, (n, 128), 1) < 64
@@ -460,6 +463,22 @@
             )
         return carry
 
+    return attend
+
+
+def backward_kernel(cap, scale, dmixed, lines, table, g, dproj, out, recv, wide128, gathered, sorter, dlines_in,
+                    dlines, wide32, back, sems, *scratch):
+    me = lax.axis_index("space")
+    count = recv.shape[0]
+    red = Reducer(me, g, out, *scratch)
+    greet_all(me, count, True)
+    send_to_lines(me, count, 1, dmixed, recv, sems.at[0], sems.at[1])
+    red.start()
+    build_sorter(table[...], sorter)
+    await_bytes(recv, sems.at[1])
+    red.step(0)
+    sort_blocks(cap, recv, wide128, gathered, sorter, dlines_in)
+    attend = backward_tiles(scale, lines, dlines_in, dlines)
     tiles = cap * count // TILE
     lax.fori_loop(0, tiles // 2, attend, 0)
     red.step(1)
@@ -513,7 +532,7 @@
         functools.partial(backward_kernel, cap, scale),
         out_shape=(
             jax.ShapeDtypeStruct((BINS, span, 1536), BF16),
-            jax.ShapeDtypeStruct((2, 3, 4, 4, q, 512), BF16),
+            jax.ShapeDtypeStruct(g.shape, BF16),
         ),
         in_specs=[VM] * 4,
         out_specs=(VM,) * 2,
@@ -531,8 +550,146 @@
         + reducer_scratch(q),
         compiler_params=pltpu.CompilerParams(collective_id=10 + cap, has_side_effects=True, vmem_limit_bytes=60 << 20),
         name="backward_lines",
-    )(dmixed, lines, table, g.reshape(2, 3, 4, 4, q, 512))
-    return dproj, out.reshape(g.shape)
+    )(dmixed, lines, table, g)
+    return dproj, out
+
+
+def step_back_kernel(scale, dmixed, lines, table, activated, upstream, normed_mlp, dpre, mixed, dhidden_b, normed, w_qkv,
+                     unit, inv, dhidden, gain, mlp_gain_sum, pack, grad_states, early, late, gains_out,
+                     recv, wide128, gathered, sorter, dlines_in, dlines, wide32, back, dproj, g, g_late, shifted, sems, *scratch):
+    me = lax.axis_index("space")
+    cap = 4
+    count = recv.shape[0]
+    red = Reducer(me, g, early, *scratch[:9])
+    red_late = Reducer(me, g_late, late, *scratch[9:18])
+    slots, held, gsend, grecv = scratch[18:]
+    gain_refs = (held, gsend, grecv)
+    greet_all(me, count, True)
+    send_to_lines(me, count, 1, dmixed, recv, sems.at[0], sems.at[1])
+
+    def blocks(j, width=512):
+        return pl.ds(pl.multiple_of(j * width, width), width)
+
+    def down_sum(j, carry):
+        g[blocks(j), :] = dot(activated[:, blocks(j)], upstream[...], TN).astype(BF16)
+        return carry
+
+    def up_sum(j, carry):
+        g[blocks(j + 4), :] = dot(normed_mlp[...], dpre[:, blocks(j)], TN).astype(BF16)
+        return carry
+
+    lax.fori_loop(0, 4, down_sum, 0)
+    lax.fori_loop(0, 4, up_sum, 0)
+    g[pl.ds(4096, 512), :] = dot(mixed[...], dhidden_b[...], TN).astype(BF16)
+    red.start()
+    build_sorter(table[...], sorter)
+    await_bytes(recv, sems.at[1])
+    sort_blocks(cap, recv, wide128, gathered, sorter, dlines_in)
+    attend = backward_tiles(scale, lines, dlines_in, dlines)
+    tiles = cap * count // TILE
+    lax.fori_loop(0, tiles // 2, attend, 0)
+    red.step(0)
+    lax.fori_loop(tiles // 2, tiles, attend, 0)
+    unsort_blocks(cap, dlines, wide32, sorter, back)
+    send_home(me, count, 3, back, dproj, sems.at[2], sems.at[3])
+    red.step(1)
+    red.step(2)
+    await_bytes(dproj, sems.at[3])
+    rows = BINS * cap * SEG
+
+    def late_sum(j, carry):
+        rhs = dproj[:, :, blocks(j)].reshape(rows, 512)
+        g_late[blocks(j), :] = dot(normed[...], rhs, TN).astype(BF16)
+        return carry
+
+    lax.fori_loop(0, 3, late_sum, 0)
+    red_late.start()
+
+    def norm_chunk(i, total):
+        part = pl.ds(pl.multiple_of(i * 128, 128), 128)
+        dn = dot(dproj[pl.ds(i * 4, 4)].reshape(128, 1536), w_qkv[...], NT).astype(BF16).astype(F32)
+        u = unit[part, :]
+        shifted[part, :] = (dhidden[part, :] + norm_back(u, inv[part, :], gain[...], dn)).astype(BF16)
+        return total + jnp.sum(u * dn, axis=0, keepdims=True)
+
+    total = lax.fori_loop(0, rows // 128, norm_chunk, jnp.zeros((1, 512), F32))
+    for j in range(4):
+        held[0, pl.ds(j, 1), :] = total[:, 128 * j : 128 * (j + 1)]
+    held[0, pl.ds(4, 4), :] = mlp_gain_sum[...]
+    sum_gains(0, red, slots, gain_refs)
+    red_late.step(0)
+    grad_states[...] = dot(pack[...], shifted[...], TN).astype(BF16)
+    for stage in range(7):
+        if stage > 0:
+            red_late.step(stage)
+        if stage == 0:
+            red.step(3)
+        if stage == 1:
+            red.step(4)
+        if stage == 2:
+            red.step(5)
+        if stage == 5:
+            red.step(6)
+        if stage < 4:
+            some = gather_gains(stage, slots, gain_refs)
+            if stage < 3:
+                held[stage + 1] = some
+                sum_gains(stage + 1, red, slots, gain_refs)
+            else:
+                gains_out[...] = some
+    for p in range(3):
+        red.wait(7, p)
+        red_late.wait(7, p)
+    red.finish()
+    red_late.finish()
+    for stage in range(4):
+        await_bytes(slots.at[stage, pl.ds(0, 1 if stage == 0 else 3)], gsend.at[stage])
+    await_bytes(recv.at[pl.ds(0, count - 1)], sems.at[0])
+    await_bytes(back.at[pl.ds(0, count - 1)], sems.at[2])
+
+
+def step_back(scale, *args):
+    cap, count = 4, 64
+    n = cap * count
+    span = cap * SEG
+    rows = BINS * span
+    out = pl.pallas_call(
+        functools.partial(step_back_kernel, scale),
+        out_shape=(
+            jax.ShapeDtypeStruct((512, 512), BF16),
+            jax.ShapeDtypeStruct((4608, 512), BF16),
+            jax.ShapeDtypeStruct((1536, 512), BF16),
+            jax.ShapeDtypeStruct((8, 128), F32),
+        ),
+        in_specs=[VM] * len(args),
+        out_specs=(VM,) * 4,
+        scratch_shapes=[
+            pltpu.VMEM((count, span, 128), BF16),
+            pltpu.VMEM((1, count * span, 128), F32),
+            pltpu.VMEM((n, 128), BF16),
+            pltpu.VMEM((n, n), BF16),
+            pltpu.VMEM((SEG, n, 128), BF16),
+            pltpu.VMEM((SEG, n, 384), BF16),
+            pltpu.VMEM((3, count * span, 128), F32),
+            pltpu.VMEM((count, span, 384), BF16),
+            pltpu.VMEM((BINS, span, 1536), BF16),
+            pltpu.VMEM((4608, 512), BF16),
+            pltpu.VMEM((1536, 512), BF16),
+            pltpu.VMEM((rows, 512), BF16),
+            pltpu.SemaphoreType.DMA((4,)),
+        ]
+        + reducer_scratch(48)
+        + reducer_scratch(16)
+        + [
+            pltpu.VMEM((4, 4, 8, 128), F32),
+            pltpu.VMEM((4, 8, 128), F32),
+            pltpu.SemaphoreType.DMA((4,)),
+            pltpu.SemaphoreType.DMA((4,)),
+        ],
+        compiler_params=pltpu.CompilerParams(collective_id=30, has_side_effects=True, vmem_limit_bytes=62 << 20),
+        name="step_back",
+    )(*args)
+    return out
 
 
 def fits_four(owner):
@@ -592,21 +749,27 @@
     dhidden = upstream.astype(F32) + norm_back(unit_m, inv_m, gain_mlp, dnormed_mlp)
     dhidden_b = dhidden.astype(BF16)
     dmixed = dot(dhidden_b, w_out, NT).astype(BF16)
-    early = [dot(activated, upstream, TN)]
-    early += [dot(normed_mlp, dpre[:, j * width : (j + 1) * width], TN) for j in range(4)]
-    early += [dot(mixed, dhidden_b, TN)]
-    early = jnp.concatenate([v.astype(BF16) for v in early], axis=0)
-
-    dprojected, early = backward_lines(dmixed.reshape(BINS, span, width), lines, table, early, cap, nspace, scale)
-    dprojected = dprojected.reshape(BINS * span, 3 * width)
-    late = [dot(normed, dprojected[:, j * width : (j + 1) * width], TN) for j in range(3)]
-    late = jnp.concatenate([v.astype(BF16) for v in late], axis=0)
-    dnormed = dot(dprojected, w_qkv, NT).astype(BF16).astype(F32)
-    grad_gain_attn = jnp.sum(unit_a * dnormed, axis=0)
-    grad_states = (dhidden + norm_back(unit_a, inv_a, gain_attn, dnormed)).astype(BF16)
     output = dot(pack, output, TN).astype(BF16)
-    grad_states = dot(pack, grad_states, TN).astype(BF16)
-    late, gains = reduce_tail(cap, late, jnp.concatenate([grad_gain_attn, grad_gain_mlp]).reshape(8, 128))
+    if cap == 4:
+        grad_states, early, late, gains = step_back(
+            scale, dmixed.reshape(BINS, span, width), lines, table, activated, upstream, normed_mlp, dpre, mixed, dhidden_b,
+            normed, w_qkv, unit_a, inv_a, dhidden, gain_attn[None], grad_gain_mlp.reshape(4, 128), pack,
+        )
+    else:
+        early = [dot(activated, upstream, TN)]
+        early += [dot(normed_mlp, dpre[:, j * width : (j + 1) * width], TN) for j in range(4)]
+        early += [dot(mixed, dhidden_b, TN)]
+        early = jnp.concatenate([v.astype(BF16) for v in early], axis=0)
+
+        dprojected, early = backward_lines(dmixed.reshape(BINS, span, width), lines, table, early, cap, nspace, scale)
+        dprojected = dprojected.reshape(BINS * span, 3 * width)
+        late = [dot(normed, dprojected[:, j * width : (j + 1) * width], TN) for j in range(3)]
+        late = jnp.concatenate([v.astype(BF16) for v in late], axis=0)
+        dnormed = dot(dprojected, w_qkv, NT).astype(BF16).astype(F32)
+        grad_gain_attn = jnp.sum(unit_a * dnormed, axis=0)
+        grad_states = (dhidden + norm_back(unit_a, inv_a, gain_attn, dnormed)).astype(BF16)
+        grad_states = dot(pack, grad_states, TN).astype(BF16)
+        late, gains = reduce_tail(cap, late, jnp.concatenate([grad_gain_attn, grad_gain_mlp]).reshape(8, 128))
     factor = 1.0 / math.sqrt(total_rows)
     gains = gains.reshape(2, width) * factor
     hidden_units = w_up.shape[1]

time: 250 us -> 218 us (0.87)
  matrix products: 41.6 us -> 25.1 us
  Pallas kernels: 172 us -> 157 us
  local copies, waits for them, and re-layouts: 2.18 us -> 9.04 us
  other arithmetic: 18.8 us -> 15.1 us
    dot_general x20 -> x9, matrix products: 41.6 us -> 25.1 us  [dot(): return lax.dot_general(a, b, (dims, ((), ())), preferred_element_type=F32)]
    pallas_call x2 -> x1, Pallas kernels: 113 us -> 98 us  [step_back(): pl.pallas_call(functools.partial(step_back_kernel, scale), out_shape=(jax...]
    unnamed x0 -> x13, local copies, waits for them, and re-layouts: none -> 4.67 us
    concatenate x2, other arithmetic: 4.26 us -> 0.57 us  [columns(): jnp.concatenate([blocks[j].astype(F32) * factor for j in range(blocks.sha...]
    convert_element_type x0 -> x3, other arithmetic: none -> 2.69 us  [the longest x1 1.44 us: block(): dhidden_b = dhidden.astype(BF16)]
where the time goes in v5:
time: 218 us; the launch traced here: 214 us
  Pallas kernels  157 us (72%)
  matrix products  25.1 us (12%)
  other arithmetic  15.1 us (7%)
  local copies, waits for them, and re-layouts  9.04 us (4%)
  loops' own time  5.44 us (2%)
  between operations  2.31 us (1%)
    pallas_call x1, Pallas kernels, step_back(): pl.pallas_call(functools.partial(step_back_kernel, scale), out_shape=(jax...  98 us
    pallas_call x1, Pallas kernels, forward_lines(): pl.pallas_call(functools.partial(forward_kernel, cap, scale), out_shape=(...  58.6 us
    dot_general x9, matrix products, dot(): return lax.dot_general(a, b, (dims, ((), ())), preferred_element_type=F32)  25.1 us
    another operation x1, loops' own time, per_device(): lax.cond(fits_four(args[2]), functools.partial(block, 4), functools.parti...  5.44 us
    unnamed x13, local copies, waits for them, and re-layouts  4.67 us

profile of v5, /device:TPU:1, one launch (start us, length us, event | category | flops | bytes accessed | tf_op | source)
XLA Modules:
  0.0 213.7 jit_solution(3676328463395747173)
XLA Ops:
  0.6 0.9 convert_reduce_fusion.8
  3.5 205.1 %conditional.1 = (bf16[1,512,512]{2,1,0:T(8,128)(2,1)}, bf16[1,512,512]{2,1,0:T(8,128)(2,1)S(1)}, f32[512]{0:T(512)S(1)}, f32[512,1536]{1,0:T(8,128)S(1)}, f32[5...) conditional(s32[]{:T(128)} %convert_element_type.232, ...), branch_computations={%region_3.20_spmd, %region_20.34_spmd} | conditional | flops 16228642816 | bytes 223168768 | solution.py:704
  6.6 0.9 convert_reduce_fusion.7
  7.5 0.9 convert_reduce_fusion.6
  11.1 1.3 fusion.134
  13.8 1.5 convolution_convert_fusion.16.upstream
  15.3 1.0 fusion.122.pack
  17.2 0.9 copy.51.inv
  18.0 1.2 fusion.105
  19.3 3.7 %convolution_convert_fusion.14 = bf16[512,1536]{1,0:T(8,128)(2,1)} fusion(bf16[512,512]{1,0:T(8,128)(2,1)S(1)} %get-tuple-element.146.normed, bf16[512,1536]{1,0:T(8,128)(2,1)} %get-tuple-element.60.w_qkv), kind=kOutput, calls=%fused_computation.166 | convolution fusion | flops 806092800 | bytes 3670016 | tf_op jit(solution)/shard_map/cond/branch_1_fun/dot_general | solution.py:24
  23.0 58.6 %forward_lines.3 = (bf16[16,32,512]{2,1,0:T(8,128)(2,1)}, bf16[8,256,384]{2,1,0:T(8,128)(2,1)}, s32[8,128]{1,0:T(8,128)}) custom-call(bf16[16,32,1536]{2,1,0:T(8,128)(2,1)} %bitcast.76, s32[16,8,128]{2,1,0:T(8,128)} %broadcast_select_fusion.1.tagt), custom_call_target="tpu_custom_call" | custom-call | tf_op jit(solution)/shard_map/cond/branch_1_fun/forward_lines/pallas_call | solution.py:502
  81.7 1.7 convert_reduce_fusion.4
  84.0 3.3 %multiply_convert_fusion.4 = (bf16[512,2048]{1,0:T(8,128)(2,1)}, f32[512,2048]{1,0:T(8,128)S(1)}) fusion(bf16[512,512]{1,0:T(8,128)(2,1)S(1)} %fusion.114.normed_mlp, bf16[512,2048]{1,0:T(8,128)(2,1)S(1)} %copy-done.27), kind=kOutput, calls=%fused_computation.164 | convolution fusion | flops 1083179008 | bytes 8912896 | tf_op jit(solution)/shard_map/cond/branch_1_fun/dot_general | solution.py:24
  87.4 4.1 %fusion.102.dpre = bf16[512,2048]{1,0:T(8,128)(2,1)} fusion(f32[512,2048]{1,0:T(8,128)S(1)} %get-tuple-element.154, bf16[512,512]{1,0:T(8,128)(2,1)S(1)} %convolution_convert_fusion.16.upstream, bf16[2048,512]{1,0:T(8,128)(2,1)S(1)} %copy-done.28), kind=kOutput, calls=%fused_computation.161 | convolution fusion | flops 1092616192 | bytes 8912896 | tf_op jit(solution)/shard_map/cond/branch_1_fun/dot_general | solution.py:24
  91.5 4.6 %fusion.113 = bf16[1,512,512]{2,1,0:T(8,128)(2,1)} fusion(bf16[512,2048]{1,0:T(8,128)(2,1)} %get-tuple-element.153.activated, bf16[2048,512]{1,0:T(8,128)(2,1)} %get-tuple-element.66, bf16[512,512]{1,0:T(8,128)(2,1)S(1)} %get-tuple-element.152, s32[512]{0:T(512)S(1)} %add.254), kind=kOutput, calls=%fused_computation.187 | convolution fusion | flops 1343488000 | bytes 5244928 | tf_op jit(solution)/shard_map/cond/branch_1_fun/dot_general | solution.py:24
  96.1 4.3 %fusion.119 = (f32[512]{0:T(512)}, f32[512]{0:T(512)S(1)}, f32[512]{0:T(512)S(1)}, f32[512,512]{1,0:T(8,128)S(1)}) fusion(bf16[512,512]{1,0:T(8,128)(2,1)S(1)} %get-tuple-element.152, f32[512]{0:T(512)S(1)} %add_rsqrt_fusion.2, f32[512]{0:T(512)S(1)} %broadcast_multiply_fusion.11, f32[512]{0:T(512)S(1)} %copy-done.19, bf16[512,2048]{1,0:T(8,128)(2,1)} %fusion.102.dpre, ...), kind=kOutput, calls=%fused_computation.193 | convolution fusion | flops 1076099584 | bytes 5779456 | tf_op jit(solution)/shard_map/cond/branch_1_fun/dot_general | solution.py:24
  100.4 1.4 fusion.137
  101.9 1.3 convolution_convert_fusion.15
  103.1 98.0 %step_back.1 = (bf16[512,512]{1,0:T(8,128)(2,1)}, bf16[4608,512]{1,0:T(8,128)(2,1)}, bf16[1536,512]{1,0:T(8,128)(2,1)}, f32[8,128]{1,0:T(8,128)}) custom-call(bf16[16,32,512]{2,1,0:T(8,128)(2,1)} %bitcast.75, bf16[8,256,384]{2,1,0:T(8,128)(2,1)} %get-tuple-element.68.lines, s32[8,128]{1,0:T(8,128)} %get-tuple-element.69.table, ...), custom_call_target="tpu_custom_call" | custom-call | tf_op jit(solution)/shard_map/cond/branch_1_fun/step_back/pallas_call | solution.py:656
  201.8 1.8 convert_multiply_fusion.19
  203.9 2.1 copy-done.1
  209.6 1.2 copy-done.2
  210.8 1.4 copy-done.3
  212.2 0.9 copy-done.4
  (65 shorter events, 8.6 us)
Async XLA Ops:
  6.5 9.8 %copy-start.30 = (bf16[1,512,512]{2,1,0:T(8,128)(2,1)S(1)}, bf16[1,512,512]{2,1,0:T(8,128)(2,1)}, u32[]{:S(2)}) copy-start(bf16[1,512,512]{2,1,0:T(8,128)(2,1)} %get-tuple-element.58) | copy-start | bytes 1572868 | tf_op jit(solution)/shard_map/cond
  13.8 4.3 %copy-start.21 = (f32[512]{0:T(512)S(1)}, f32[512]{0:T(512)}, u32[]{:S(2)}) copy-start(f32[512]{0:T(512)} %get-tuple-element.59) | copy-start | bytes 6148 | tf_op jit(solution)/shard_map/cond
  15.3 85.1 %copy-start.5 = (bf16[512,512]{1,0:T(8,128)(2,1)}, bf16[512,512]{1,0:T(8,128)(2,1)S(1)}, u32[]{:S(2)}) copy-start(bf16[512,512]{1,0:T(8,128)(2,1)S(1)} %convolution_convert_fusion.16.upstream) | copy-start | bytes 1572868 | tf_op jit(solution)/shard_map/cond
  19.3 3.8 %copy-start.6 = (bf16[512,512]{1,0:T(8,128)(2,1)}, bf16[512,512]{1,0:T(8,128)(2,1)S(1)}, u32[]{:S(2)}) copy-start(bf16[512,512]{1,0:T(8,128)(2,1)S(1)} %get-tuple-element.146.normed) | copy-start | bytes 1572868 | tf_op jit(solution)/shard_map/cond
  19.3 62.4 %copy-start.9 = (bf16[512,512]{1,0:T(8,128)(2,1)S(1)}, bf16[512,512]{1,0:T(8,128)(2,1)}, u32[]{:S(2)}) copy-start(bf16[512,512]{1,0:T(8,128)(2,1)} %get-tuple-element.63) | copy-start | bytes 1572868 | tf_op jit(solution)/shard_map/cond
  23.0 60.7 %copy-start.19 = (f32[512]{0:T(512)S(1)}, f32[512]{0:T(512)}, u32[]{:S(2)}) copy-start(f32[512]{0:T(512)} %get-tuple-element.64) | copy-start | bytes 6148 | tf_op jit(solution)/shard_map/cond
  81.7 2.3 %copy-start.27 = (bf16[512,2048]{1,0:T(8,128)(2,1)S(1)}, bf16[512,2048]{1,0:T(8,128)(2,1)}, u32[]{:S(2)}) copy-start(bf16[512,2048]{1,0:T(8,128)(2,1)} %get-tuple-element.65) | copy-start | bytes 6291460 | tf_op jit(solution)/shard_map/cond
  84.0 3.4 %copy-start.7 = (bf16[512,512]{1,0:T(8,128)(2,1)}, bf16[512,512]{1,0:T(8,128)(2,1)S(1)}, u32[]{:S(2)}) copy-start(bf16[512,512]{1,0:T(8,128)(2,1)S(1)} %fusion.114.normed_mlp) | copy-start | bytes 1572868 | tf_op jit(solution)/shard_map/cond
  84.0 3.4 %copy-start.28 = (bf16[2048,512]{1,0:T(8,128)(2,1)S(1)}, bf16[2048,512]{1,0:T(8,128)(2,1)}, u32[]{:S(2)}) copy-start(bf16[2048,512]{1,0:T(8,128)(2,1)} %get-tuple-element.66) | copy-start | bytes 6291460 | tf_op jit(solution)/shard_map/cond
  100.4 1.5 copy-start.10
  101.9 1.3 copy-start
  203.6 2.3 %copy-start.1 = (bf16[4608,512]{1,0:T(8,128)(2,1)S(1)}, bf16[4608,512]{1,0:T(8,128)(2,1)}, u32[]{:S(2)}) copy-start(bf16[4608,512]{1,0:T(8,128)(2,1)} %get-tuple-element.73) | copy-start | bytes 14155780 | tf_op jit(solution)/shard_map/cond
  207.3 1.1 copy-start.17
  208.6 2.2 %copy-start.2 = (f32[2048,512]{1,0:T(8,128)}, f32[2048,512]{1,0:T(8,128)S(1)}, u32[]{:S(2)}) copy-start(f32[2048,512]{1,0:T(8,128)S(1)} %get-tuple-element.189) | copy-start | bytes 12582916
  208.6 3.5 %copy-start.3 = (f32[512,2048]{1,0:T(8,128)}, f32[512,2048]{1,0:T(8,128)S(1)}, u32[]{:S(2)}) copy-start(f32[512,2048]{1,0:T(8,128)S(1)} %get-tuple-element.188) | copy-start | bytes 12582916
  208.7 4.4 %copy-start.4 = (f32[512,1536]{1,0:T(8,128)}, f32[512,1536]{1,0:T(8,128)S(1)}, u32[]{:S(2)}) copy-start(f32[512,1536]{1,0:T(8,128)S(1)} %get-tuple-element.185) | copy-start | bytes 9437188
  208.7 4.7 %copy-start.13 = (f32[512,512]{1,0:T(8,128)}, f32[512,512]{1,0:T(8,128)S(1)}, u32[]{:S(2)}) copy-start(f32[512,512]{1,0:T(8,128)S(1)} %get-tuple-element.186) | copy-start | bytes 3145732
  208.7 4.7 %copy-start.22 = (f32[512]{0:T(512)}, f32[512]{0:T(512)S(1)}, u32[]{:S(2)}) copy-start(f32[512]{0:T(512)S(1)} %get-tuple-element.187) | copy-start | bytes 6148
  208.7 4.7 %copy-start.23 = (f32[512]{0:T(512)}, f32[512]{0:T(512)S(1)}, u32[]{:S(2)}) copy-start(f32[512]{0:T(512)S(1)} %get-tuple-element.184) | copy-start | bytes 6148
